TPU v7x, 128 devices: a whole 4x4x4 slice. The times are simulated.
128 devices in a mesh: frame: 32 (over x, y, z_lo), row: 4 (over z_hi, core).
Axes of the slice: x: 4, y: 4, z: 4 (z_hi: 2, z_lo: 2; z = z_hi * 2 + z_lo), core: 2. Of those that a mesh axis runs over, the one named last changes fastest.
Arguments:
- query_pre: bfloat16 [2240, 32, 16, 128], P(None, 'frame', 'row'), may hold values from -6 to 6
- key_pre: bfloat16 [2240, 32, 16, 128], P(None, 'frame', 'row'), may hold values from -80 to 80
- values: bfloat16 [2240, 32, 16, 128], P(None, 'frame', 'row'), may hold values from -1 to 2
- cotangent: bfloat16 [2240, 32, 16, 128], P(None, 'frame', 'row'), may hold values from -3072 to 3072
- kernel: bfloat16 [3, 3, 2240], replicated, may hold values from -0.29882812 to 0.59765625
Outputs:
- grad_query: bfloat16 [2240, 32, 16, 128], P(None, 'frame', 'row')
- grad_key: bfloat16 [2240, 32, 16, 128], P(None, 'frame', 'row')
- grad_values: bfloat16 [2240, 32, 16, 128], P(None, 'frame', 'row')
All inputs are finite; a program needn't handle non-finite values.
Results may differ from a plain program's by a relative error of at most 0.008.
Values may be sent and summed in bfloat16 or wider, within the bound.
A program may use at most 128 MiB of HBM per device.

v0:
```python
import jax
import jax.numpy as jnp
from jax import lax
from jax.sharding import PartitionSpec as P

HD = 32


denominator_eps = 0.001


def extended(array, sides, width):
    for axis, dim in sides:
        size, length = (lax.axis_size(axis), array.shape[dim])
        up = [(i, (i + 1) % size) for i in range(size - 1)]
        down = [(j, i) for i, j in up]
        last = lax.slice_in_dim(array, length - width, length, axis=dim)
        leading = lax.slice_in_dim(array, 0, width, axis=dim)
        before = lax.ppermute(last, axis, up)
        after = lax.ppermute(leading, axis, down)
        array = jnp.concatenate([before, array, after], axis=dim)
    return array


def conv_taps(padded, weights, flipped, row_count, col_count):
    summed = None
    for tap_row in range(3):
        for tap_col in range(3):
            start_row = 2 - tap_row if flipped else tap_row
            start_col = 2 - tap_col if flipped else tap_col
            window = padded[
                :, :, start_row : start_row + row_count, start_col : start_col + col_count
            ]
            tap_term = weights[tap_row, tap_col][:, None, None, None] * window
            summed = tap_term if summed is None else summed + tap_term
    return summed


def pad_columns(field):
    return jnp.pad(field, ((0, 0), (0, 0), (0, 0), (1, 1)))


def shards(query_pre, key_pre, values, cotangent, kernel):
    highest = lax.Precision.HIGHEST
    channels, frames, row_count, col_count = values.shape
    head_count = channels // HD
    tokens_dev = frames * row_count * col_count
    all_tokens = tokens_dev * lax.axis_size("frame") * lax.axis_size("row")
    flat = (head_count, HD, tokens_dev)
    weights = kernel.astype(jnp.float32)
    value_ext = extended(values, (("row", 2),), 1)
    value_pad = pad_columns(value_ext.astype(jnp.float32))
    mixed = conv_taps(value_pad, weights, False, row_count, col_count).reshape(flat)
    key_act = jax.nn.relu(key_pre.astype(jnp.float32)).reshape(flat)
    query_act = jax.nn.relu(query_pre.astype(jnp.float32)).reshape(flat)
    local_state = jnp.einsum("hjt,het->hje", key_act, mixed, precision=highest)
    local_sum = jnp.sum(key_act, axis=2)
    state, key_sum = lax.psum((local_state, local_sum), ("frame", "row"))
    denom = (
        jnp.einsum("hj,hjt->ht", key_sum, query_act, precision=highest)
        + denominator_eps * all_tokens
    )
    numer = jnp.einsum("hje,hjt->het", state, query_act, precision=highest)
    output = numer / denom[:, None, :]
    grad_out = cotangent.astype(jnp.float32).reshape(flat)
    grad_num = grad_out / denom[:, None, :]
    grad_den = -jnp.sum(grad_out * output, axis=1) / denom
    local_gstate = jnp.einsum("hjt,het->hje", query_act, grad_num, precision=highest)
    local_gsum = jnp.einsum("hjt,ht->hj", query_act, grad_den, precision=highest)
    grad_state, grad_sum = lax.psum((local_gstate, local_gsum), ("frame", "row"))
    grad_qact = (
        jnp.einsum("hje,het->hjt", state, grad_num, precision=highest)
        + key_sum[:, :, None] * grad_den[:, None, :]
    )
    grad_query = (
        jnp.where(query_pre.reshape(flat) > 0, grad_qact, 0.0)
        .astype(jnp.bfloat16)
        .reshape(values.shape)
    )
    grad_mixed = jnp.einsum("hje,hjt->het", grad_state, key_act, precision=highest)
    grad_kact = (
        jnp.einsum("hje,het->hjt", grad_state, mixed, precision=highest) + grad_sum[:, :, None]
    )
    grad_key = (
        jnp.where(key_pre.reshape(flat) > 0, grad_kact, 0.0)
        .astype(jnp.bfloat16)
        .reshape(values.shape)
    )
    grad_grid = grad_mixed.reshape(channels, frames, row_count, col_count)
    grad_ext = extended(grad_grid.astype(jnp.bfloat16), (("row", 2),), 1).astype(grad_grid.dtype)
    grad_values = conv_taps(pad_columns(grad_ext), weights, True, row_count, col_count).astype(
        jnp.bfloat16
    )
    return (grad_query, grad_key, grad_values)


def solution(mesh):
    return jax.shard_map(
        shards,
        mesh=mesh,
        in_specs=(
            P(None, "frame", "row", None),
            P(None, "frame", "row", None),
            P(None, "frame", "row", None),
            P(None, "frame", "row", None),
            P(),
        ),
        out_specs=(
            P(None, "frame", "row", None),
            P(None, "frame", "row", None),
            P(None, "frame", "row", None),
        ),
        check_vma=False,
    )
```

profile of v0, /device:TPU:1, one launch (start us, length us, event | category | flops | bytes accessed | tf_op | source)
XLA Modules:
  0.0 554.9 jit_solution(3331773693273662485)
XLA Ops:
  7.2 0.0 all-reduce.5.cloned.1.call-start
  7.2 4.5 fusion.36
  11.7 0.9 copy.42
  12.6 3.4 collective-permute-start.1
  16.0 0.9 copy.41
  16.9 5.5 collective-permute-start
  22.4 5.1 reshape.172
  27.6 18.0 %fusion.30 = (f32[2240]{0:T(1024)S(1)}, f32[2240,1,4,128]{3,2,1,0:T(4,128)}) fusion(bf16[2240,1,4,128]{3,2,1,0:T(4,128)(2,1)S(1)} %copy-done.2), kind=kLoop, calls=%fused_computation.59 | loop fusion | flops 3438400 | bytes 6890240 | tf_op jit(solution)/shard_map/reduce_sum | solution.py:57
  45.5 6.3 %reshape.164 = f32[70,32,512]{2,1,0:T(8,128)} reshape(f32[2240,1,4,128]{3,2,1,0:T(4,128)} %get-tuple-element.26) | data formatting | bytes 9175040 | tf_op jit(solution)/shard_map/reshape | solution.py:54
  51.9 0.8 slice_reduce_fusion.8
  52.7 4.6 convert_maximum_fusion
  57.3 6.3 %reshape.168 = f32[70,32,512]{2,1,0:T(8,128)} reshape(f32[2240,1,4,128]{3,2,1,0:T(4,128)} %convert_maximum_fusion) | data formatting | bytes 9175040 | tf_op jit(solution)/shard_map/reshape | solution.py:55
  63.6 0.1 reduce_sum.21
  63.7 65.3 %psum.29 = f32[70,32]{1,0:T(8,128)S(1)} all-reduce(f32[70,32]{1,0:T(8,128)S(1)} %reduce_sum.21), channel_id=1, replica_groups=mesh['frame'=32,'row'=4] {'frame','row'}, use_global_device_ids=true, to_apply=%region_2.3 | all-reduce | flops 2240 | bytes 17920 | tf_op jit(solution)/shard_map/psum | solution.py:58
  129.1 4.8 fusion.33
  133.8 0.7 copy-done.5
  134.5 8.0 %fusion.29 = f32[70,32,32]{2,1,0:T(8,128)} fusion(f32[70,32,512]{2,1,0:T(8,128)S(1)} %copy-done, f32[70,32,512]{2,1,0:T(8,128)} %reshape.172, f32[70,512]{1,0:T(8,128)S(1)} %bitcast_add_fusion), kind=kOutput, calls=%fused_computation.56 | convolution fusion | flops 441548800 | bytes 9605120 | tf_op jit(solution)/shard_map/hjt,het->hje/dot_general | solution.py:68
  142.5 1.5 broadcast_compare_fusion.1
  144.1 5.7 %copy.25 = bf16[2240,1,1,128]{3,2,1,0:T(2,128)(2,1)S(1)} copy(bf16[2240,1,1,128]{3,0,2,1:T(8,128)(2,1)} %collective-permute-done.1) | data formatting | bytes 1146880 | tf_op jit(solution)/shard_map/ppermute | solution.py:20
  149.8 5.9 %copy.24 = bf16[2240,1,1,128]{3,2,1,0:T(2,128)(2,1)S(1)} copy(bf16[2240,1,1,128]{3,0,2,1:T(8,128)(2,1)} %collective-permute-done) | data formatting | bytes 1146880 | tf_op jit(solution)/shard_map/ppermute | solution.py:19
  155.8 3.6 maximum_convert_fusion
  159.5 41.7 %fusion.8 = f32[2240,1,4,128]{3,2,1,0:T(4,128)} fusion(f32[2240,1,6,128]{3,2,1,0:T(8,128)S(1)} %maximum_convert_fusion, f32[2240]{0:T(1024)S(1)} %get-tuple-element.13, f32[2240]{0:T(1024)S(1)} %get-tuple-element.14, f32[2240]{0:T(1024)S(1)} %get-tuple-element.15, f32[2240]{0:T(1024)S(1)} %get-tuple-element.16, f32[2240]{0:T(1024)S(1)} %get-tuple-element.17, ...), kind=kLoop, calls=%fused_computation.20 | loop fusion | flops 19496960 | bytes 27635712 | tf_op jit(solution)/shard_map/add | solution.py:35
  201.2 6.3 %reshape.165 = f32[70,32,512]{2,1,0:T(8,128)} reshape(f32[2240,1,4,128]{3,2,1,0:T(4,128)} %fusion.8) | data formatting | bytes 9175040 | tf_op jit(solution)/shard_map/reshape | solution.py:53
  207.5 9.0 %fusion.37 = f32[70,32,32]{2,1,0:T(8,128)} fusion(f32[70,32,512]{2,1,0:T(8,128)} %reshape.164, f32[70,32,512]{2,1,0:T(8,128)} %reshape.165), kind=kOutput, calls=%fused_computation.78 | convolution fusion | flops 440401920 | bytes 9461760 | tf_op jit(solution)/shard_map/hjt,het->hje/dot_general | solution.py:56
  216.5 0.0 all-reduce.5.cloned.1.call-update
  216.5 2.5 broadcast_compare_fusion
  219.0 3.3 gt.13
  222.3 4.8 gt.15
  227.1 138.8 %all-reduce.5.cloned.1.call-done = (f32[70,32,32]{2,1,0:T(8,128)}, f32[70,32,32]{2,1,0:T(8,128)}) async-done(((f32[70,32,32]{2,1,0:T(8,128)}, f32[70,32,32]{2,1,0:T(8,128)}), (f32[70,32,32]{2,1,0:T(8,128)}, f32[70,32,32]{2,1,0:T(8,128)})) %all-reduce.5.cloned.1.call-update) | async-done | bytes 573456 | tf_op jit(solution)/shard_map/psum | solution.py:58
  365.9 8.2 %multiply_reduce_fusion = f32[70,512]{1,0:T(8,128)S(1)} fusion(f32[70,32,512]{2,1,0:T(8,128)} %reshape.172, f32[70,32,32]{2,1,0:T(8,128)} %get-tuple-element.21, f32[70,32,512]{2,1,0:T(8,128)} %reshape.168, f32[70,512]{1,0:T(8,128)S(1)} %copy-done.10), kind=kOutput, calls=%fused_computation.50 | convolution fusion | flops 443806720 | bytes 9748480 | tf_op jit(solution)/shard_map/hje,hjt->het/dot_general | solution.py:63
  374.1 0.7 negate_divide_fusion
  374.9 5.2 convolution_convert_fusion
  380.0 4.1 convert_element_type.73
  384.2 1.7 fusion.35
  385.9 0.9 copy.44
  386.8 2.9 collective-permute-start.3
  389.7 0.9 copy.43
  390.6 4.4 collective-permute-start.2
  395.1 8.6 %select_convert_fusion.1 = bf16[70,32,512]{2,1,0:T(8,128)(2,1)} fusion(pred[70,32,512]{2,1,0:T(32,128)(4,1)S(1)} %copy-done.7, f32[70,512]{1,0:T(8,128)S(1)} %copy-done.8, f32[70,32]{1,0:T(8,128)S(1)} %psum.29, f32[70,32,32]{2,1,0:T(8,128)S(1)} %copy-done.25, f32[70,32,512]{2,1,0:T(8,128)} %reshape.172, f32[70,512]{1,0:T(8,128)S(1)} %copy-done.11), kind=kOutput, calls=%fused_computation.49 | convolution fusion | flops 446136320 | bytes 8610560 | tf_op jit(solution)/shard_map/hje,het->hjt/dot_general | solution.py:72
  403.7 4.1 fusion.31
  407.7 5.1 reshape.169
  412.9 64.3 %psum.31 = f32[70,32]{1,0:T(8,128)S(1)} all-reduce(f32[70,32]{1,0:T(8,128)S(1)} %bitcast.32), channel_id=1, replica_groups=mesh['frame'=32,'row'=4] {'frame','row'}, use_global_device_ids=true, to_apply=%region_5.6 | all-reduce | flops 2240 | bytes 17920 | tf_op jit(solution)/shard_map/psum | solution.py:70
  477.2 8.6 %select_convert_fusion = bf16[70,32,512]{2,1,0:T(8,128)(2,1)} fusion(pred[70,32,512]{2,1,0:T(32,128)(4,1)S(1)} %gt.15, f32[70,32]{1,0:T(8,128)S(1)} %psum.31, f32[70,32,32]{2,1,0:T(8,128)} %get-tuple-element.22, f32[70,32,512]{2,1,0:T(8,128)} %reshape.165), kind=kOutput, calls=%fused_computation.48 | convolution fusion | flops 443842560 | bytes 8323840 | tf_op jit(solution)/shard_map/hje,het->hjt/dot_general | solution.py:82
  485.8 5.1 reshape.170
  490.9 5.7 %copy.32 = bf16[2240,1,1,128]{3,2,1,0:T(2,128)(2,1)S(1)} copy(bf16[2240,1,1,128]{3,0,2,1:T(8,128)(2,1)} %collective-permute-done.3) | data formatting | bytes 1146880 | tf_op jit(solution)/shard_map/ppermute | solution.py:20
  496.7 5.7 %copy.30 = bf16[2240,1,1,128]{3,2,1,0:T(2,128)(2,1)S(1)} copy(bf16[2240,1,1,128]{3,0,2,1:T(8,128)(2,1)} %collective-permute-done.2) | data formatting | bytes 1146880 | tf_op jit(solution)/shard_map/ppermute | solution.py:19
  502.5 3.6 maximum_convert_fusion.1
  506.2 41.7 %fusion.28 = bf16[2240,1,4,128]{3,2,1,0:T(4,128)(2,1)} fusion(f32[2240,1,6,128]{3,2,1,0:T(8,128)S(1)} %maximum_convert_fusion.1, f32[2240]{0:T(1024)S(1)} %get-tuple-element.13, f32[2240]{0:T(1024)S(1)} %get-tuple-element.14, f32[2240]{0:T(1024)S(1)} %copy-done.13, f32[2240]{0:T(1024)S(1)} %copy-done.15, f32[2240]{0:T(1024)S(1)} %copy-done.17, ...), kind=kLoop, calls=%fused_computation.53 | loop fusion | flops 20643840 | bytes 25341952 | tf_op jit(solution)/shard_map/convert_element_type | solution.py:91
  (68 shorter events, 0.2 us)
Async XLA Ops:
  7.2 358.7 %all-reduce.5.cloned.1.call-start = ((), (), s32[]{:S(2)}) async-start(), calls=%async_computation | async-start | bytes 4587520 | tf_op jit(solution)/shard_map/psum | solution.py:58
  12.6 14.9 %copy-start.2 = (bf16[2240,1,4,128]{3,2,1,0:T(4,128)(2,1)S(1)}, bf16[2240,1,4,128]{3,2,1,0:T(4,128)(2,1)}, u32[]{:S(2)}) copy-start(bf16[2240,1,4,128]{3,2,1,0:T(4,128)(2,1)} %param.6) | copy-start | bytes 6881284
  12.6 131.5 %collective-permute-start.1 = (bf16[2240,1,1,128]{3,0,2,1:T(8,128)(2,1)}, bf16[2240,1,1,128]{3,0,2,1:T(8,128)(2,1)}, u32[]{:S(2)}, u32[]{:S(2)}) collective-permute-start(bf16[2240,1,1,128]{3,0,2,1:T(8,128)(2,1)} %copy.42), channel_id=1, source_target_pairs={{1,0},{2,1},{3,2},{5,4},{6,5},{7,6},{9,8},{10,9},{11,10},{13,12},{... | collective-permute-start | bytes 1720328 | tf_op jit(solution)/shard_map/ppermute | solution.py:20
  16.9 132.9 %collective-permute-start = (bf16[2240,1,1,128]{3,0,2,1:T(8,128)(2,1)}, bf16[2240,1,1,128]{3,0,2,1:T(8,128)(2,1)}, u32[]{:S(2)}, u32[]{:S(2)}) collective-permute-start(bf16[2240,1,1,128]{3,0,2,1:T(8,128)(2,1)} %copy.41), channel_id=1, source_target_pairs={{0,1},{1,2},{2,3},{4,5},{5,6},{6,7},{8,9},{9,10},{10,11},{12,13},{... | collective-permute-start | bytes 1720328 | tf_op jit(solution)/shard_map/ppermute | solution.py:19
  45.5 6.3 %copy-start.24 = (bf16[3,3,2240]{2,1,0:T(4,128)(2,1)S(1)}, bf16[3,3,2240]{2,1,0:T(4,128)(2,1)}, u32[]{:S(2)}) copy-start(bf16[3,3,2240]{2,1,0:T(4,128)(2,1)} %param.9) | copy-start | bytes 120964
  52.7 106.8 %copy-start.12 = (f32[2240]{0:T(1024)}, f32[2240]{0:T(1024)S(1)}, u32[]{:S(2)}) copy-start(f32[2240]{0:T(1024)S(1)} %get-tuple-element.15) | copy-start | bytes 26884
  52.7 106.8 %copy-start.14 = (f32[2240]{0:T(1024)}, f32[2240]{0:T(1024)S(1)}, u32[]{:S(2)}) copy-start(f32[2240]{0:T(1024)S(1)} %get-tuple-element.16) | copy-start | bytes 26884
  52.7 106.8 %copy-start.16 = (f32[2240]{0:T(1024)}, f32[2240]{0:T(1024)S(1)}, u32[]{:S(2)}) copy-start(f32[2240]{0:T(1024)S(1)} %get-tuple-element.17) | copy-start | bytes 26884
  129.1 5.5 copy-start
  133.8 0.7 copy-start.5
  134.5 8.0 %copy-start.9 = (f32[70,512]{1,0:T(8,128)}, f32[70,512]{1,0:T(8,128)S(1)}, u32[]{:S(2)}) copy-start(f32[70,512]{1,0:T(8,128)S(1)} %bitcast_add_fusion) | copy-start | bytes 430084
  134.5 8.0 %copy-start.3 = (bf16[2240,1,4,128]{3,2,1,0:T(4,128)(2,1)S(1)}, bf16[2240,1,4,128]{3,2,1,0:T(4,128)(2,1)}, u32[]{:S(2)}) copy-start(bf16[2240,1,4,128]{3,2,1,0:T(4,128)(2,1)} %param.5) | copy-start | bytes 6881284
  142.5 13.2 %copy-start.1 = (bf16[2240,1,4,128]{3,2,1,0:T(4,128)(2,1)S(1)}, bf16[2240,1,4,128]{3,2,1,0:T(4,128)(2,1)}, u32[]{:S(2)}) copy-start(bf16[2240,1,4,128]{3,2,1,0:T(4,128)(2,1)} %param.7) | copy-start | bytes 6881284
  155.8 3.7 copy-start.18
  155.8 3.7 copy-start.20
  155.8 3.7 copy-start.22
  219.0 146.9 %copy-start.10 = (f32[70,512]{1,0:T(8,128)S(1)}, f32[70,512]{1,0:T(8,128)}, u32[]{:S(2)}) copy-start(f32[70,512]{1,0:T(8,128)} %copy-done.9) | copy-start | bytes 430084
  222.3 152.6 %slice-start.2 = ((s8[4587520]{0:T(1024)(128)(4,1)}), s8[393216]{0:T(1024)(128)(4,1)S(1)}, s32[]{:S(2)}) async-start(s8[4587520]{0:T(1024)(128)(4,1)} %bitcast.26), calls=%async_computation.3 | async-start | bytes 786432
  365.9 8.2 %copy-start.6 = (f32[70,1,512]{2,1,0:T(1,128)S(1)}, f32[70,1,512]{2,1,0:T(1,128)}, u32[]{:S(2)}) copy-start(f32[70,1,512]{2,1,0:T(1,128)} %copy-done.5) | copy-start | bytes 430084
  365.9 8.9 %slice-start.3 = ((s8[4587520]{0:T(1024)(128)(4,1)}), s8[4194304]{0:T(1024)(128)(4,1)S(1)}, s32[]{:S(2)}) async-start(s8[4587520]{0:T(1024)(128)(4,1)} %bitcast.26), calls=%async_computation.4 | async-start | bytes 8388608
  365.9 8.9 %copy-start.4 = (f32[70,32,32]{2,1,0:T(8,128)S(1)}, f32[70,32,32]{2,1,0:T(8,128)}, u32[]{:S(2)}) copy-start(f32[70,32,32]{2,1,0:T(8,128)} %get-tuple-element.22) | copy-start | bytes 860164
  384.2 10.9 %copy-start.7 = (pred[70,32,512]{2,1,0:T(32,128)(4,1)S(1)}, pred[70,32,512]{2,1,0:T(32,128)(4,1)}, u32[]{:S(2)}) copy-start(pred[70,32,512]{2,1,0:T(32,128)(4,1)} %gt.13) | copy-start | bytes 3440644
  384.2 10.9 %copy-start.8 = (f32[70,512]{1,0:T(8,128)S(1)}, f32[70,512]{1,0:T(8,128)}, u32[]{:S(2)}) copy-start(f32[70,512]{1,0:T(8,128)} %negate_divide_fusion) | copy-start | bytes 430084
  384.2 10.9 %copy-start.11 = (f32[70,512]{1,0:T(8,128)S(1)}, f32[70,512]{1,0:T(8,128)}, u32[]{:S(2)}) copy-start(f32[70,512]{1,0:T(8,128)} %copy-done.9) | copy-start | bytes 430084
  384.2 10.9 %copy-start.25 = (f32[70,32,32]{2,1,0:T(8,128)S(1)}, f32[70,32,32]{2,1,0:T(8,128)}, u32[]{:S(2)}) copy-start(f32[70,32,32]{2,1,0:T(8,128)} %get-tuple-element.21) | copy-start | bytes 860164
  386.8 104.2 %collective-permute-start.3 = (bf16[2240,1,1,128]{3,0,2,1:T(8,128)(2,1)}, bf16[2240,1,1,128]{3,0,2,1:T(8,128)(2,1)}, u32[]{:S(2)}, u32[]{:S(2)}) collective-permute-start(bf16[2240,1,1,128]{3,0,2,1:T(8,128)(2,1)} %copy.44), channel_id=1, source_target_pairs={{1,0},{2,1},{3,2},{5,4},{6,5},{7,6},{9,8},{10,9},{11,10},{13,12},{... | collective-permute-start | bytes 1720328 | tf_op jit(solution)/shard_map/ppermute | solution.py:20
  389.7 13.9 %slice-start = ((s8[4587520]{0:T(1024)(128)(4,1)}), s8[4194304]{0:T(1024)(128)(4,1)S(1)}, s32[]{:S(2)}) async-start(s8[4587520]{0:T(1024)(128)(4,1)} %bitcast.24), calls=%async_computation.1 | async-start | bytes 8388608
  390.6 13.0 %slice-start.1 = ((s8[4587520]{0:T(1024)(128)(4,1)}), s8[393216]{0:T(1024)(128)(4,1)S(1)}, s32[]{:S(2)}) async-start(s8[4587520]{0:T(1024)(128)(4,1)} %bitcast.24), calls=%async_computation.2 | async-start | bytes 786432
  390.6 106.1 %collective-permute-start.2 = (bf16[2240,1,1,128]{3,0,2,1:T(8,128)(2,1)}, bf16[2240,1,1,128]{3,0,2,1:T(8,128)(2,1)}, u32[]{:S(2)}, u32[]{:S(2)}) collective-permute-start(bf16[2240,1,1,128]{3,0,2,1:T(8,128)(2,1)} %copy.43), channel_id=1, source_target_pairs={{0,1},{1,2},{2,3},{4,5},{5,6},{6,7},{8,9},{9,10},{10,11},{12,13},{... | collective-permute-start | bytes 1720328 | tf_op jit(solution)/shard_map/ppermute | solution.py:19
  502.4 3.7 copy-start.13
  502.4 3.7 copy-start.15
  502.4 3.7 copy-start.17
  502.4 3.7 copy-start.19
  502.4 3.7 copy-start.21
  502.5 3.7 copy-start.23
Sparse Core Ops, SparseCore 0:
  216.6 149.2 all-reduce.4
where the time goes:
time: 562 us; the launch traced here: 555 us
  waiting for transfers between devices  139 us (25%)
  blocking collectives  130 us (23%)
  other arithmetic  118 us (21%)
  local copies, waits for them, and re-layouts  81 us (14%)
  matrix products  56.3 us (10%)
  starting transfers between devices  16.3 us (3%)
  between operations  14.7 us (3%)
    psum x1, waiting for transfers between devices, shards(): state, key_sum = lax.psum((local_state, local_sum), ('frame', 'row'))  139 us
    psum x1, blocking collectives, shards(): state, key_sum = lax.psum((local_state, local_sum), ('frame', 'row'))  65.3 us
    psum x1, blocking collectives, shards(): lax.psum((local_gstate, local_gsum), ('frame', 'row'))  64.3 us
    convert_element_type x1, other arithmetic, shards(): conv_taps(pad_columns(grad_ext), weights, True, row_count, col_count)  41.7 us
    add x1, other arithmetic, conv_taps(): summed = tap_term if summed is None else summed + tap_term  41.7 us
    reduce_sum x1, other arithmetic, shards(): local_sum = jnp.sum(key_act, axis=2)  18 us
    ppermute x2, local copies, waits for them, and re-layouts, extended(): before = lax.ppermute(last, axis, up)  11.7 us
    ppermute x2, local copies, waits for them, and re-layouts, extended(): after = lax.ppermute(leading, axis, down)  11.4 us
  transfers between devices with their start and end apart: 5, of which 1 were waited for; matrix products, arithmetic and copies ran while one was open for 20% of the time, Pallas kernels for 0%

commit v1 on v0

v1 whole, which is shorter than its diff:
```python
import functools

import jax
import jax.numpy as jnp
from jax import lax
from jax.experimental import pallas as pl
from jax.experimental.pallas import tpu as pltpu
from jax.sharding import PartitionSpec as P

HD = 32
HPG = 7
GC = HPG * HD
GK = 256
COLS = 128
ROWS = 4
UNITS = 16
EPS = 0.001
MESH = pl.DeviceIdType.MESH
F32 = jnp.float32
BF16 = jnp.bfloat16


def lanes(shape):
    return lax.broadcasted_iota(jnp.int32, shape, len(shape) - 1)


def conv16(rows, weights, flipped):
    lane = lanes((16, COLS))
    taps = [jnp.broadcast_to(weights[:, i : i + 1], (16, COLS)) for i in range(9)]
    outs = []
    for r in range(ROWS):
        sums = []
        for b in range(3):
            total = None
            for a in range(3):
                at = (2 - a) * 3 + (2 - b) if flipped else a * 3 + b
                term = taps[at] * rows[r + a]
                total = term if total is None else total + term
            sums.append(total)
        before = jnp.where(lane >= 1, pltpu.roll(sums[0], 1, 1), 0.0)
        after = jnp.where(lane < COLS - 1, pltpu.roll(sums[2], COLS - 1, 1), 0.0)
        outs.append(sums[1] + before + after)
    return outs


def pack(full):
    lane = lanes((HD, 128))
    block = lax.shift_right_logical(lane, 5)
    first = jnp.zeros((HD, 128), F32)
    second = jnp.zeros((HD, 128), F32)
    for h in range(HPG):
        rows = slice(HD * h, HD * h + HD)
        if h < 4:
            first = jnp.where(block == h, full[rows, :128], first)
        else:
            second = jnp.where(block == h - 4, full[rows, 128:], second)
        second = jnp.where(lane == 96 + h, full[rows, 128:], second)
    return first, second


def put_units(ref, at, packed):
    for t, part in enumerate(packed):
        for k in range(8):
            ref[at + t * 8 + k] = part[4 * k : 4 * k + 4]


def take_units(ref, at):
    halves = [
        jnp.concatenate([ref[at + t * 8 + k] for k in range(8)], axis=0) for t in range(2)
    ]
    return jnp.concatenate(halves, axis=1)


def spread(packed, keep_sums):
    stacked = jnp.concatenate([packed] * HPG, axis=0)
    head = lax.shift_right_logical(lax.broadcasted_iota(jnp.int32, (GC, GK), 0), 5)
    lane = lanes((GC, GK))
    keep = head == lax.shift_right_logical(lane, 5)
    if keep_sums:
        keep = keep | (lane == GC + head)
    return jnp.where(keep, stacked, 0.0)


def first_kernel(
    frames, rows, all_tokens,
    q_hbm, k_hbm, v_hbm, c_hbm, w_ref,
    state_out, mixed_out, key_out, query_out, weights_out,
    qn, kn, vn, cn, wide, vpl, vedge, vhalo, kp, qp, cp, mf, mx, wt,
    part1, part2, got1, got2, all1, all2, means, qout,
    in_sem, out_sem, vsend, vrecv, ksend, krecv, s_sem, r_sem, g_sem, a_sem,
):
    groups = vpl.shape[0] // GC
    n_dev = frames * rows
    frame, row = lax.axis_index("frame"), lax.axis_index("row")
    me = frame * rows + row
    has_up, has_down = row > 0, row < rows - 1
    n_units = groups * UNITS
    extra = n_units - n_dev

    def device(d):
        return (d // rows, lax.rem(d, rows))

    sources = ((v_hbm, vn), (k_hbm, kn), (q_hbm, qn), (c_hbm, cn))

    def load(i, g):
        src, dst = sources[i]
        at = pl.ds(pl.multiple_of(g * GC * ROWS, GC * ROWS), GC * ROWS)
        return pltpu.make_async_copy(src.at[at], dst.at[at], in_sem.at[i, g])

    for i in range(4):

        @pl.loop(0, groups)
        def _(g):
            load(i, g).start()

    barrier = pltpu.get_barrier_semaphore()

    @pl.loop(1, n_dev)
    def _(i):
        d = lax.rem(me + i, n_dev)
        pl.semaphore_signal(barrier, inc=1, device_id=device(d), device_id_type=MESH)

    taps = jnp.concatenate([w_ref[a].astype(F32) for a in range(3)], axis=0)
    taps = jnp.concatenate([taps, jnp.zeros((7, taps.shape[1]), F32)], axis=0)
    channels = taps.shape[1]
    for at in range(0, channels, 128):
        size = min(128, channels - at)
        wt[at : at + size, :] = jnp.concatenate(
            [taps[:, at : at + size].T, jnp.zeros((size, 112), F32)], axis=1
        )

    def planes(nat, g):
        at = pl.multiple_of(g * GC * ROWS, GC * ROWS)
        wide[...] = nat[pl.ds(at, GC * ROWS), :].astype(F32)
        return [wide[pl.ds(r, GC, stride=ROWS), :] for r in range(ROWS)]

    def at_group(g, size=GC):
        return pl.ds(pl.multiple_of(g * size, size), size)

    @pl.loop(0, groups)
    def _(g):
        load(0, g).wait()
        rows4 = planes(vn, g)
        for r in range(ROWS):
            vpl[at_group(g), COLS * r : COLS * r + COLS] = rows4[r]
        vedge[0, at_group(g), :] = rows4[0].astype(BF16)
        vedge[1, at_group(g), :] = rows4[3].astype(BF16)

    zero_plane = jnp.zeros((GC, COLS), BF16)

    @pl.when(jnp.logical_not(has_up))
    def _():
        @pl.loop(0, groups)
        def _(g):
            vhalo[0, at_group(g), :] = zero_plane
            kp[at_group(g), 0:COLS] = zero_plane

    @pl.when(jnp.logical_not(has_down))
    def _():
        @pl.loop(0, groups)
        def _(g):
            vhalo[1, at_group(g), :] = zero_plane
            kp[at_group(g), 5 * COLS : 6 * COLS] = zero_plane

    pl.semaphore_wait(barrier, n_dev - 1)

    def value_halo(way, g):
        return pltpu.make_async_remote_copy(
            src_ref=vedge.at[way, at_group(g), :],
            dst_ref=vhalo.at[1 - way, at_group(g), :],
            send_sem=vsend.at[way],
            recv_sem=vrecv.at[1 - way, g],
            device_id=(frame, row - 1 if way == 0 else row + 1),
            device_id_type=MESH,
        )

    def key_halo(way, g):
        src = COLS if way == 0 else 4 * COLS
        dst = 5 * COLS if way == 0 else 0
        return pltpu.make_async_remote_copy(
            src_ref=kp.at[at_group(g), src : src + COLS],
            dst_ref=kp.at[at_group(g), dst : dst + COLS],
            send_sem=ksend.at[way],
            recv_sem=krecv.at[1 - way, g],
            device_id=(frame, row - 1 if way == 0 else row + 1),
            device_id_type=MESH,
        )

    def send_halos(halo):
        for way, there in ((0, has_up), (1, has_down)):

            @pl.when(there)
            def _():
                @pl.loop(0, groups)
                def _(g):
                    halo(way, g).start()

    def wait_halo(halo, g):
        for way, there in ((1, has_up), (0, has_down)):

            @pl.when(there)
            def _():
                halo(way, g).wait_recv()

    def wait_sent(sem):
        for way, there in ((0, has_up), (1, has_down)):

            @pl.when(there)
            def _():
                pltpu.make_async_copy(vedge.at[way], vedge.at[way], sem.at[way]).wait()

    send_halos(value_halo)

    @pl.loop(0, groups)
    def _(g):
        load(1, g).wait()
        rows4 = planes(kn, g)
        for r in range(ROWS):
            kp[at_group(g), COLS * (r + 1) : COLS * (r + 2)] = jnp.maximum(
                rows4[r], 0.0
            ).astype(BF16)
        mx[pl.ds(pl.multiple_of(g * GK + GC, 32), GK - GC), :] = jnp.ones(
            (GK - GC, ROWS * COLS), BF16
        )

    @pl.loop(0, groups)
    def _(g):
        load(2, g).wait()
        rows4 = planes(qn, g)
        for r in range(ROWS):
            qp[at_group(g), COLS * r : COLS * (r + 1)] = jnp.maximum(rows4[r], 0.0).astype(BF16)

    @pl.loop(0, groups)
    def _(g):
        load(3, g).wait()
        rows4 = planes(cn, g)
        top = pl.ds(pl.multiple_of(g * GK, GK), GC)
        for r in range(ROWS):
            cp[top, COLS * r : COLS * (r + 1)] = rows4[r].astype(BF16)
        cp[pl.ds(pl.multiple_of(g * GK + GC, 32), GK - GC), :] = jnp.zeros(
            (GK - GC, ROWS * COLS), BF16
        )

    def owner(u):
        f = u - n_dev
        second = u >= n_dev
        return jnp.where(second, f * rows + lax.rem(f, rows), u), jnp.where(second, 1, 0)

    owns_two = (row == lax.rem(frame, rows)) & (frame < extra)
    second_unit = n_dev + frame

    def scatter(part, got, at, g):
        @pl.loop(0, UNITS)
        def _(i):
            u = g * UNITS + i
            d, slot = owner(u)

            @pl.when(d != me)
            def _():
                pltpu.make_async_remote_copy(
                    src_ref=part.at[u],
                    dst_ref=got.at[slot * n_dev + me],
                    send_sem=s_sem.at[at],
                    recv_sem=r_sem.at[at, slot],
                    device_id=device(d),
                    device_id_type=MESH,
                ).start()

            @pl.when(d == me)
            def _():
                got[slot * n_dev + me] = part[u]

    def wait_bytes(ref, count, sem):
        pltpu.make_async_copy(ref.at[pl.ds(0, count)], ref.at[pl.ds(0, count)], sem).wait()

    def gather(got, every, at):
        def one(slot, u):
            wait_bytes(got, n_dev - 1, r_sem.at[at, slot])
            every[u] = jnp.sum(got[slot * n_dev : (slot + 1) * n_dev], axis=0)

            @pl.loop(1, n_dev)
            def _(i):
                d = lax.rem(me + i, n_dev)
                pltpu.make_async_remote_copy(
                    src_ref=every.at[u],
                    dst_ref=every.at[u],
                    send_sem=g_sem.at[at],
                    recv_sem=a_sem.at[at, slot],
                    device_id=device(d),
                    device_id_type=MESH,
                ).start()

        one(0, me)

        @pl.when(owns_two)
        def _():
            one(1, second_unit)

    def wait_gathered(every, at):
        wait_bytes(every, n_dev - 1, a_sem.at[at, 0])

        @pl.when(owns_two)
        def _():
            wait_bytes(every, extra - 1, a_sem.at[at, 1])

        @pl.when(jnp.logical_not(owns_two))
        def _():
            wait_bytes(every, extra, a_sem.at[at, 1])

    def wait_sends(at):
        @pl.when(owns_two)
        def _():
            wait_bytes(part1, n_units - 2, s_sem.at[at])
            wait_bytes(got1, 2 * (n_dev - 1), g_sem.at[at])

        @pl.when(jnp.logical_not(owns_two))
        def _():
            wait_bytes(part1, n_units - 1, s_sem.at[at])
            wait_bytes(got1, n_dev - 1, g_sem.at[at])

    @pl.loop(0, groups)
    def _(g):
        wait_halo(value_halo, g)

        @pl.loop(0, GC // 16)
        def _(i):
            c = pl.ds(pl.multiple_of(g * GC + i * 16, 16), 16)
            six = [vhalo[0, c, :].astype(F32)]
            six += [vpl[c, COLS * r : COLS * (r + 1)] for r in range(ROWS)]
            six += [vhalo[1, c, :].astype(F32)]
            outs = conv16(six, wt[c, :], False)
            o = pl.ds(pl.multiple_of(g * GK + i * 16, 16), 16)
            for r in range(ROWS):
                mf[c, COLS * r : COLS * (r + 1)] = outs[r]
                mx[o, COLS * r : COLS * (r + 1)] = outs[r].astype(BF16)

        full = lax.dot_general(
            kp[at_group(g), COLS : 5 * COLS],
            mx[at_group(g, GK), :],
            (((1,), (1,)), ((), ())),
            preferred_element_type=F32,
        )
        put_units(part1, g * UNITS, pack(full))
        scatter(part1, got1, 0, g)

    send_halos(key_halo)
    weights_copy = pltpu.make_async_copy(wt, weights_out, out_sem.at[0])
    weights_copy.start()
    gather(got1, all1, 0)
    wait_gathered(all1, 0)

    @pl.loop(0, groups)
    def _(g):
        packed = take_units(all1, g * UNITS)
        lane = lanes((HD, GK))
        head = lax.shift_right_logical(lane, 5)
        sums = [packed[:, GC + h : GC + h + 1] for h in range(HPG)]
        sums_wide = jnp.zeros((HD, GK), F32)
        for h in range(HPG):
            sums_wide = jnp.where(head == h, sums[h], sums_wide)
        total = jnp.sum(packed, axis=0, keepdims=True)
        weight = jnp.sum(sums_wide, axis=0, keepdims=True)
        mean = total / (weight + EPS * all_tokens)
        mean = jnp.where(lanes((1, GK)) < GC, mean, 0.0)
        means[g] = jnp.broadcast_to(mean, (8, GK))
        centred = spread(packed - sums_wide * mean, False)
        mean_rows = jnp.where(
            lax.shift_right_logical(lanes((16, GK)), 5)
            == lax.broadcasted_iota(jnp.int32, (16, GK), 0),
            mean,
            0.0,
        )
        left = jnp.concatenate([centred, mean_rows], axis=0).astype(BF16)
        cot = cp[at_group(g, GK), :]
        prod = jnp.dot(left, cot, preferred_element_type=F32)
        stacked = jnp.concatenate([jnp.broadcast_to(s, (HD, 128)) for s in sums], axis=0)
        by_head = jnp.where(
            lanes((GC, 128))
            == lax.shift_right_logical(lax.broadcasted_iota(jnp.int32, (GC, 128), 0), 5),
            stacked,
            0.0,
        )
        sums_rows = by_head.T[:16]
        high = sums_rows.astype(BF16)
        low = (sums_rows - high.astype(F32)).astype(BF16)
        qa = qp[at_group(g), :]
        both = jnp.dot(
            jnp.concatenate([high, low], axis=0), qa, preferred_element_type=F32
        )
        denom = both[:16] + both[16:] + EPS * all_tokens
        inv = 1.0 / denom
        down_rows = []
        scaled = []
        for h in range(HPG):
            rows_h = slice(HD * h, HD * h + HD)
            qh = qa[rows_h].astype(F32)
            ph = prod[rows_h]
            dot_h = jnp.sum(qh * ph, axis=0, keepdims=True)
            inv_h = inv[h : h + 1]
            down = -(dot_h - EPS * all_tokens * prod[GC + h : GC + h + 1]) * inv_h
            down_rows.append(down)
            grad = ph * inv_h + stacked[rows_h, 0:1] * (down * inv_h)
            grad = jnp.where(qh > 0, grad, 0.0)
            scaled.append((qh * inv_h).astype(BF16))
            for r in range(ROWS):
                wide[pl.ds(h * HD * ROWS + r, HD, stride=ROWS), :] = grad[
                    :, COLS * r : COLS * (r + 1)
                ]
        nat = pl.ds(pl.multiple_of(g * GC * ROWS, GC * ROWS), GC * ROWS)
        qout[nat, :] = wide[...].astype(BF16)
        tail = jnp.concatenate(down_rows + [jnp.zeros((GK - GC - HPG, ROWS * COLS), F32)], axis=0)
        right = jnp.concatenate([cot[:GC], tail.astype(BF16)], axis=0)
        full = lax.dot_general(
            jnp.concatenate(scaled, axis=0),
            right,
            (((1,), (1,)), ((), ())),
            preferred_element_type=F32,
        )
        put_units(part2, g * UNITS, pack(full))
        scatter(part2, got2, 1, g)

    query_copy = pltpu.make_async_copy(qout, query_out, out_sem.at[1])
    query_copy.start()

    @pl.loop(0, groups)
    def _(g):
        column = means[g].T[:GC, 0:1]
        o = pl.ds(pl.multiple_of(g * GK, GK), GC)
        mx[o, :] = (mf[at_group(g), :] - column).astype(BF16)
        wait_halo(key_halo, g)

    mixed_copy = pltpu.make_async_copy(mx, mixed_out, out_sem.at[2])
    mixed_copy.start()
    key_copy = pltpu.make_async_copy(kp, key_out, out_sem.at[3])
    key_copy.start()

    gather(got2, all2, 1)
    wait_gathered(all2, 1)
    state_copy = pltpu.make_async_copy(all2, state_out, out_sem.at[4])
    state_copy.start()
    wait_sent(vsend)
    wait_sent(ksend)
    wait_sends(0)
    wait_sends(1)
    weights_copy.wait()
    query_copy.wait()
    mixed_copy.wait()
    key_copy.wait()
    state_copy.wait()


def second_kernel(state, mixed, keys, weights, query_in, gq, gk, gv, wide, mapped):
    gq[...] = query_in[...]
    packed = take_units(state, 0)
    left = spread(packed, True).astype(BF16)
    grad_key = jnp.dot(left, mixed[...], preferred_element_type=F32)
    for r in range(ROWS):
        part = grad_key[:, COLS * r : COLS * (r + 1)]
        wide[pl.ds(r, GC, stride=ROWS), :] = jnp.where(
            keys[:, COLS * (r + 1) : COLS * (r + 2)].astype(F32) > 0, part, 0.0
        )
    gk[...] = wide[...].astype(BF16)
    turned = jnp.concatenate([packed] * 4, axis=0).T[:GC]
    turned = jnp.concatenate([turned, turned], axis=1)
    head = lax.shift_right_logical(lax.broadcasted_iota(jnp.int32, (GC, GK), 0), 5)
    turned = jnp.where(head == lax.shift_right_logical(lanes((GC, GK)), 5), turned, 0.0)
    mapped[...] = jnp.dot(
        turned[:, :GC].astype(BF16), keys[...], preferred_element_type=F32
    )

    @pl.loop(0, GC // 16)
    def _(i):
        c = pl.ds(pl.multiple_of(i * 16, 16), 16)
        six = [mapped[c, COLS * r : COLS * (r + 1)] for r in range(ROWS + 2)]
        outs = conv16(six, weights[c, :], True)
        for r in range(ROWS):
            wide[pl.ds(i * 16 * ROWS + r, 16, stride=ROWS), :] = outs[r]

    gv[...] = wide[...].astype(BF16)


def shards(frames, rows, query_pre, key_pre, values, cotangent, kernel):
    channels = values.shape[0]
    groups = channels // GC
    flat = (channels * ROWS, COLS)
    tokens = ROWS * COLS
    all_tokens = tokens * frames * rows
    n_units = groups * UNITS
    n_dev = frames * rows
    hbm = pl.BlockSpec(memory_space=pl.ANY)
    unit = (4, 128)
    state, mixed, keys, query, weights = pl.pallas_call(
        functools.partial(first_kernel, frames, rows, all_tokens),
        out_shape=(
            jax.ShapeDtypeStruct((n_units, *unit), F32),
            jax.ShapeDtypeStruct((groups * GK, tokens), BF16),
            jax.ShapeDtypeStruct((channels, 6 * COLS), BF16),
            jax.ShapeDtypeStruct(flat, BF16),
            jax.ShapeDtypeStruct((channels, 128), F32),
        ),
        in_specs=[hbm] * 4 + [pl.BlockSpec(memory_space=pltpu.VMEM)],
        out_specs=(hbm,) * 5,
        scratch_shapes=[
            pltpu.VMEM(flat, BF16),
            pltpu.VMEM(flat, BF16),
            pltpu.VMEM(flat, BF16),
            pltpu.VMEM(flat, BF16),
            pltpu.VMEM((GC * ROWS, COLS), F32),
            pltpu.VMEM((channels, tokens), F32),
            pltpu.VMEM((2, channels, COLS), BF16),
            pltpu.VMEM((2, channels, COLS), BF16),
            pltpu.VMEM((channels, 6 * COLS), BF16),
            pltpu.VMEM((channels, tokens), BF16),
            pltpu.VMEM((groups * GK, tokens), BF16),
            pltpu.VMEM((channels, tokens), F32),
            pltpu.VMEM((groups * GK, tokens), BF16),
            pltpu.VMEM((channels, 128), F32),
            pltpu.VMEM((n_units, *unit), F32),
            pltpu.VMEM((n_units, *unit), F32),
            pltpu.VMEM((2 * n_dev, *unit), F32),
            pltpu.VMEM((2 * n_dev, *unit), F32),
            pltpu.VMEM((n_units, *unit), F32),
            pltpu.VMEM((n_units, *unit), F32),
            pltpu.VMEM((groups, 8, GK), F32),
            pltpu.VMEM(flat, BF16),
            pltpu.SemaphoreType.DMA((4, groups)),
            pltpu.SemaphoreType.DMA((5,)),
            pltpu.SemaphoreType.DMA((2,)),
            pltpu.SemaphoreType.DMA((2, groups)),
            pltpu.SemaphoreType.DMA((2,)),
            pltpu.SemaphoreType.DMA((2, groups)),
            pltpu.SemaphoreType.DMA((2,)),
            pltpu.SemaphoreType.DMA((2, 2)),
            pltpu.SemaphoreType.DMA((2,)),
            pltpu.SemaphoreType.DMA((2, 2)),
        ],
        compiler_params=pltpu.CompilerParams(
            collective_id=0, has_side_effects=True, vmem_limit_bytes=56 * 2**20
        ),
    )(
        query_pre.reshape(flat),
        key_pre.reshape(flat),
        values.reshape(flat),
        cotangent.reshape(flat),
        kernel,
    )
    nat = pl.BlockSpec((GC * ROWS, COLS), lambda g: (g, 0))
    gq, gk, gv = pl.pallas_call(
        second_kernel,
        grid=(groups,),
        out_shape=(jax.ShapeDtypeStruct(flat, BF16),) * 3,
        in_specs=[
            pl.BlockSpec((UNITS, *unit), lambda g: (g, 0, 0)),
            pl.BlockSpec((GK, tokens), lambda g: (g, 0)),
            pl.BlockSpec((GC, 6 * COLS), lambda g: (g, 0)),
            pl.BlockSpec((GC, 128), lambda g: (g, 0)),
            nat,
        ],
        out_specs=(nat,) * 3,
        scratch_shapes=[
            pltpu.VMEM((GC * ROWS, COLS), F32),
            pltpu.VMEM((GC, 6 * COLS), F32),
        ],
    )(state, mixed, keys, weights, query)
    return tuple(o.reshape(values.shape) for o in (gq, gk, gv))


def solution(mesh):
    frames, rows = mesh.shape["frame"], mesh.shape["row"]
    spec = P(None, "frame", "row", None)
    return jax.shard_map(
        functools.partial(shards, frames, rows),
        mesh=mesh,
        in_specs=(spec, spec, spec, spec, P()),
        out_specs=(spec, spec, spec),
        check_vma=False,
    )
```

time: 562 us -> 115 us (0.20); the launches traced: 555 us -> 115 us
  waiting for transfers between devices: 139 us -> 0 us
  blocking collectives: 130 us -> 0 us
  other arithmetic: 118 us -> 0 us
  Pallas kernels: 0 us -> 114 us
  local copies, waits for them, and re-layouts: 81 us -> 0 us
  matrix products: 56.3 us -> 0 us
  starting transfers between devices: 16.3 us -> 0 us
  between operations: 14.7 us -> 0.64 us
    psum x1 -> x0, waiting for transfers between devices: 139 us -> none  [shards(): state, key_sum = lax.psum((local_state, local_sum), ('frame', 'row'))]
    psum x2 -> x0, blocking collectives: 130 us -> none  [the longest x1 65.3 us: shards(): state, key_sum = lax.psum((local_state, local_sum), ('frame', 'row'))]
    pallas_call x0 -> x2, Pallas kernels: none -> 114 us  [the longest x1 85.6 us: shards(): pl.pallas_call(functools.partial(first_kernel, frames, rows, all_tokens),...]
    dot_general x8 -> x0, matrix products: 56.3 us -> none  [the longest x1 8.97 us: shards(): local_state = jnp.einsum('hjt,het->hje', key_act, mixed, precision=highest)]
    convert_element_type x4 -> x0, other arithmetic: 49 us -> none  [the longest x1 41.7 us: shards(): conv_taps(pad_columns(grad_ext), weights, True, row_count, col_count)]
    add x2 -> x0, other arithmetic: 41.7 us -> none  [the longest x1 41.7 us: conv_taps(): summed = tap_term if summed is None else summed + tap_term]
    reshape x6 -> x0, local copies, waits for them, and re-layouts: 34.3 us -> none  [the longest x1 6.34 us: shards(): key_act = jax.nn.relu(key_pre.astype(jnp.float32)).reshape(flat)]
    ppermute x4 -> x0, local copies, waits for them, and re-layouts: 23.1 us -> none  [the longest x2 11.7 us: extended(): before = lax.ppermute(last, axis, up)]
  transfers between devices with their start and end apart: 5 -> 0, of which waited for: 1 -> 0; matrix products, arithmetic and copies ran while one was open for 20% -> 0% of each run, Pallas kernels for 0% -> 0%
where the time goes in v1:
time: 115 us
  Pallas kernels  114 us (99%)
    pallas_call x1, Pallas kernels, shards(): pl.pallas_call(functools.partial(first_kernel, frames, rows, all_tokens),...  85.6 us
    pallas_call x1, Pallas kernels, shards(): pl.pallas_call(second_kernel, grid=(groups,), out_shape=(jax.ShapeDtypeSt...  28.8 us

profile of v1, /device:TPU:1, one launch (start us, length us, event | category | flops | bytes accessed | tf_op | source)
XLA Modules:
  0.0 115.0 jit_solution(18394017424462659475)
XLA Ops:
  0.6 85.6 %shard_map.76 = (f32[160,4,128]{2,1,0:T(4,128)}, bf16[2560,512]{1,0:T(8,128)(2,1)}, bf16[2240,768]{1,0:T(8,128)(2,1)}, bf16[8960,128]{1,0:T(8,128)(2,1)}, f32[2240,128]{1,0:T(8,128)}) custom-call(bf16[8960,128]{1,0:T(8,128)(2,1)} %bitcast.13, bf16[8960,128]{1,0:T(8,128)(2,1)} %bitcast.14, bf16[8960,128]{1,0:T(8,128)(2,1)} %bitcast.15, ...), custom_call_target="tpu_custom_call" | custom-call | tf_op jit(solution)/shard_map/pallas_call | solution.py:492
  86.2 28.8 %shard_map.77 = (bf16[8960,128]{1,0:T(8,128)(2,1)}, bf16[8960,128]{1,0:T(8,128)(2,1)}, bf16[8960,128]{1,0:T(8,128)(2,1)}) custom-call(f32[160,4,128]{2,1,0:T(4,128)} %get-tuple-element.11.state, bf16[2560,512]{1,0:T(8,128)(2,1)} %get-tuple-element.12.mixed, bf16[2240,768]{1,0:T(8,128)(2,1)} %get-tuple-element.13.keys, ...), custom_call_target="tpu_custom_call" | custom-call | tf_op jit(solution)/shard_map/pallas_call | solution.py:548

commit v2 on v1

--- a/solution.py
+++ b/solution.py
@@ -15,7 +15,9 @@
 ROWS = 4
 UNITS = 16
 EPS = 0.001
+UNROLL = 14
 MESH = pl.DeviceIdType.MESH
+FLAT = pl.DeviceIdType.LOGICAL
 F32 = jnp.float32
 BF16 = jnp.bfloat16
 
@@ -26,7 +28,11 @@
 
 def conv16(rows, weights, flipped):
     lane = lanes((16, COLS))
-    taps = [jnp.broadcast_to(weights[:, i : i + 1], (16, COLS)) for i in range(9)]
+    taps = [weights[:, COLS * i : COLS * i + COLS].astype(F32) for i in range(9)]
+    for i in range(9):
+        b = 2 - i % 3 if flipped else i % 3
+        if b != 1:
+            taps[i] = jnp.where(lane == (COLS - 1 if b == 0 else 0), 0.0, taps[i])
     outs = []
     for r in range(ROWS):
         sums = []
@@ -37,9 +43,7 @@
                 term = taps[at] * rows[r + a]
                 total = term if total is None else total + term
             sums.append(total)
-        before = jnp.where(lane >= 1, pltpu.roll(sums[0], 1, 1), 0.0)
-        after = jnp.where(lane < COLS - 1, pltpu.roll(sums[2], COLS - 1, 1), 0.0)
-        outs.append(sums[1] + before + after)
+        outs.append(sums[1] + pltpu.roll(sums[0], 1, 1) + pltpu.roll(sums[2], COLS - 1, 1))
     return outs
 
 
@@ -85,9 +89,9 @@
     frames, rows, all_tokens,
     q_hbm, k_hbm, v_hbm, c_hbm, w_ref,
     state_out, mixed_out, key_out, query_out, weights_out,
-    qn, kn, vn, cn, wide, vpl, vedge, vhalo, kp, qp, cp, mf, mx, wt,
+    qn, kn, vn, cn, wide, vpl, vedge, vhalo, kp, qp, cp, mf, mx, wt, wb, hot, sums, invs, downs,
     part1, part2, got1, got2, all1, all2, means, qout,
-    in_sem, out_sem, vsend, vrecv, ksend, krecv, s_sem, r_sem, g_sem, a_sem,
+    here, in_sem, out_sem, vsend, vrecv, ksend, krecv, s_sem, r_sem, g_sem, a_sem,
 ):
     groups = vpl.shape[0] // GC
     n_dev = frames * rows
@@ -97,8 +101,17 @@
     n_units = groups * UNITS
     extra = n_units - n_dev
 
-    def device(d):
-        return (d // rows, lax.rem(d, rows))
+    def others(act):
+        def one(i):
+            d = me + i
+            act(jnp.where(d >= n_dev, d - n_dev, d))
+
+        @pl.loop(0, (n_dev - 2) // 9)
+        def _(step):
+            for i in range(9):
+                one(step * 9 + i + 1)
+
+        one(n_dev - 1)
 
     sources = ((v_hbm, vn), (k_hbm, kn), (q_hbm, qn), (c_hbm, cn))
 
@@ -115,19 +128,17 @@
 
     barrier = pltpu.get_barrier_semaphore()
 
-    @pl.loop(1, n_dev)
-    def _(i):
-        d = lax.rem(me + i, n_dev)
-        pl.semaphore_signal(barrier, inc=1, device_id=device(d), device_id_type=MESH)
-
-    taps = jnp.concatenate([w_ref[a].astype(F32) for a in range(3)], axis=0)
-    taps = jnp.concatenate([taps, jnp.zeros((7, taps.shape[1]), F32)], axis=0)
-    channels = taps.shape[1]
-    for at in range(0, channels, 128):
-        size = min(128, channels - at)
-        wt[at : at + size, :] = jnp.concatenate(
-            [taps[:, at : at + size].T, jnp.zeros((size, 112), F32)], axis=1
-        )
+    lines = ((1, rows), (rows, 2), (2 * rows, 4), (8 * rows, 4))
+
+    def signal_line(sem, line):
+        stride, length = line
+        at = lax.rem(me // stride, length)
+        for i in range(1, length):
+            to = me + (lax.rem(at + i, length) - at) * stride
+            pl.semaphore_signal(sem, inc=1, device_id=to, device_id_type=FLAT)
+
+    for line in lines:
+        signal_line(barrier, line)
 
     def planes(nat, g):
         at = pl.multiple_of(g * GC * ROWS, GC * ROWS)
@@ -162,7 +173,8 @@
             vhalo[1, at_group(g), :] = zero_plane
             kp[at_group(g), 5 * COLS : 6 * COLS] = zero_plane
 
-    pl.semaphore_wait(barrier, n_dev - 1)
+    pl.semaphore_wait(barrier, sum(length - 1 for _, length in lines))
+    signal_line(here.at[0], lines[1])
 
     def value_halo(way, g):
         return pltpu.make_async_remote_copy(
@@ -223,6 +235,149 @@
             (GK - GC, ROWS * COLS), BF16
         )
 
+    taps = jnp.concatenate([w_ref[a].astype(F32) for a in range(3)], axis=0)
+    taps = jnp.concatenate([taps, jnp.zeros((7, taps.shape[1]), F32)], axis=0)
+    channels = taps.shape[1]
+    for at in range(0, channels, 128):
+        size = min(128, channels - at)
+        wt[at : at + size, :] = jnp.concatenate(
+            [taps[:, at : at + size].T, jnp.zeros((size, 112), F32)], axis=1
+        )
+
+    tap_of = lax.shift_right_logical(lanes((128, 9 * COLS)), 7)
+    hot[...] = jnp.where(
+        tap_of == lax.broadcasted_iota(jnp.int32, (128, 9 * COLS), 0), 1.0, 0.0
+    ).astype(BF16)
+
+    @pl.loop(0, groups)
+    def _(g):
+        wb[at_group(g), :] = jnp.dot(
+            wt[at_group(g), :].astype(BF16), hot[...], preferred_element_type=F32
+        ).astype(BF16)
+
+    weights_copy = pltpu.make_async_copy(wb, weights_out, out_sem.at[0])
+    weights_copy.start()
+
+    for i in range(1, 4):
+        pl.semaphore_wait(here.at[i - 1], lines[i][1] - 1)
+        if i < 3:
+            signal_line(here.at[i], lines[i + 1])
+
+    owns_two = (row == lax.rem(frame, rows)) & (frame < extra)
+    second_unit = n_dev + frame
+
+    def scatter(part, got, at, g):
+        second = g * UNITS >= n_dev
+        slot = jnp.where(second, 1, 0)
+        start = jnp.where(second, (g * UNITS - n_dev) * rows, g * UNITS)
+        there = slot * n_dev + me
+
+        def send(i):
+            u = g * UNITS + i
+            d = start + jnp.where(second, i * rows + i % rows, i)
+            return d, pltpu.make_async_remote_copy(
+                src_ref=part.at[u],
+                dst_ref=got.at[there],
+                send_sem=s_sem.at[at],
+                recv_sem=r_sem.at[at, slot],
+                device_id=d,
+                device_id_type=FLAT,
+            )
+
+        last = (n_dev // UNITS) - 1
+        mine = jnp.where(g > last, frame // UNITS + last + 1, me // UNITS) == g
+        mine = mine & ((g <= last) | owns_two)
+
+        @pl.when(mine)
+        def _():
+            @pl.loop(0, UNITS)
+            def _(i):
+                d, copy = send(i)
+
+                @pl.when(d != me)
+                def _():
+                    copy.start()
+
+        @pl.when(jnp.logical_not(mine))
+        def _():
+            for i in range(UNITS):
+                send(i)[1].start()
+
+    def wait_bytes(ref, count, sem):
+        pltpu.make_async_copy(ref.at[pl.ds(0, count)], ref.at[pl.ds(0, count)], sem).wait()
+
+    def gather(part, got, every, at):
+        def one(slot, u):
+            wait_bytes(got, n_dev - 1, r_sem.at[at, slot])
+            got[slot * n_dev + me] = part[u]
+            every[u] = jnp.sum(got[slot * n_dev : (slot + 1) * n_dev], axis=0)
+
+            def send(d):
+                pltpu.make_async_remote_copy(
+                    src_ref=every.at[u],
+                    dst_ref=every.at[u],
+                    send_sem=g_sem.at[at],
+                    recv_sem=a_sem.at[at, slot],
+                    device_id=d,
+                    device_id_type=FLAT,
+                ).start()
+
+            others(send)
+
+        one(0, me)
+
+        @pl.when(owns_two)
+        def _():
+            one(1, second_unit)
+
+    def wait_gathered(every, at):
+        wait_bytes(every, n_dev - 1, a_sem.at[at, 0])
+
+        @pl.when(owns_two)
+        def _():
+            wait_bytes(every, extra - 1, a_sem.at[at, 1])
+
+        @pl.when(jnp.logical_not(owns_two))
+        def _():
+            wait_bytes(every, extra, a_sem.at[at, 1])
+
+    def wait_sends(at):
+        @pl.when(owns_two)
+        def _():
+            wait_bytes(part1, n_units - 2, s_sem.at[at])
+            wait_bytes(got1, 2 * (n_dev - 1), g_sem.at[at])
+
+        @pl.when(jnp.logical_not(owns_two))
+        def _():
+            wait_bytes(part1, n_units - 1, s_sem.at[at])
+            wait_bytes(got1, n_dev - 1, g_sem.at[at])
+
+    @pl.loop(0, groups)
+    def _(g):
+        wait_halo(value_halo, g)
+
+        @pl.loop(0, GC // 16, unroll=UNROLL)
+        def _(i):
+            c = pl.ds(pl.multiple_of(g * GC + i * 16, 16), 16)
+            six = [vhalo[0, c, :].astype(F32)]
+            six += [vpl[c, COLS * r : COLS * (r + 1)] for r in range(ROWS)]
+            six += [vhalo[1, c, :].astype(F32)]
+            outs = conv16(six, wb[c, :], False)
+            o = pl.ds(pl.multiple_of(g * GK + i * 16, 16), 16)
+            for r in range(ROWS):
+                mf[c, COLS * r : COLS * (r + 1)] = outs[r]
+                mx[o, COLS * r : COLS * (r + 1)] = outs[r].astype(BF16)
+
+        full = lax.dot_general(
+            kp[at_group(g), COLS : 5 * COLS],
+            mx[at_group(g, GK), :],
+            (((1,), (1,)), ((), ())),
+            preferred_element_type=F32,
+        )
+        put_units(part1, g * UNITS, pack(full))
+        scatter(part1, got1, 0, g)
+
+    send_halos(key_halo)
     @pl.loop(0, groups)
     def _(g):
         load(2, g).wait()
@@ -241,112 +396,7 @@
             (GK - GC, ROWS * COLS), BF16
         )
 
-    def owner(u):
-        f = u - n_dev
-        second = u >= n_dev
-        return jnp.where(second, f * rows + lax.rem(f, rows), u), jnp.where(second, 1, 0)
-
-    owns_two = (row == lax.rem(frame, rows)) & (frame < extra)
-    second_unit = n_dev + frame
-
-    def scatter(part, got, at, g):
-        @pl.loop(0, UNITS)
-        def _(i):
-            u = g * UNITS + i
-            d, slot = owner(u)
-
-            @pl.when(d != me)
-            def _():
-                pltpu.make_async_remote_copy(
-                    src_ref=part.at[u],
-                    dst_ref=got.at[slot * n_dev + me],
-                    send_sem=s_sem.at[at],
-                    recv_sem=r_sem.at[at, slot],
-                    device_id=device(d),
-                    device_id_type=MESH,
-                ).start()
-
-            @pl.when(d == me)
-            def _():
-                got[slot * n_dev + me] = part[u]
-
-    def wait_bytes(ref, count, sem):
-        pltpu.make_async_copy(ref.at[pl.ds(0, count)], ref.at[pl.ds(0, count)], sem).wait()
-
-    def gather(got, every, at):
-        def one(slot, u):
-            wait_bytes(got, n_dev - 1, r_sem.at[at, slot])
-            every[u] = jnp.sum(got[slot * n_dev : (slot + 1) * n_dev], axis=0)
-
-            @pl.loop(1, n_dev)
-            def _(i):
-                d = lax.rem(me + i, n_dev)
-                pltpu.make_async_remote_copy(
-                    src_ref=every.at[u],
-                    dst_ref=every.at[u],
-                    send_sem=g_sem.at[at],
-                    recv_sem=a_sem.at[at, slot],
-                    device_id=device(d),
-                    device_id_type=MESH,
-                ).start()
-
-        one(0, me)
-
-        @pl.when(owns_two)
-        def _():
-            one(1, second_unit)
-
-    def wait_gathered(every, at):
-        wait_bytes(every, n_dev - 1, a_sem.at[at, 0])
-
-        @pl.when(owns_two)
-        def _():
-            wait_bytes(every, extra - 1, a_sem.at[at, 1])
-
-        @pl.when(jnp.logical_not(owns_two))
-        def _():
-            wait_bytes(every, extra, a_sem.at[at, 1])
-
-    def wait_sends(at):
-        @pl.when(owns_two)
-        def _():
-            wait_bytes(part1, n_units - 2, s_sem.at[at])
-            wait_bytes(got1, 2 * (n_dev - 1), g_sem.at[at])
-
-        @pl.when(jnp.logical_not(owns_two))
-        def _():
-            wait_bytes(part1, n_units - 1, s_sem.at[at])
-            wait_bytes(got1, n_dev - 1, g_sem.at[at])
-
-    @pl.loop(0, groups)
-    def _(g):
-        wait_halo(value_halo, g)
-
-        @pl.loop(0, GC // 16)
-        def _(i):
-            c = pl.ds(pl.multiple_of(g * GC + i * 16, 16), 16)
-            six = [vhalo[0, c, :].astype(F32)]
-            six += [vpl[c, COLS * r : COLS * (r + 1)] for r in range(ROWS)]
-            six += [vhalo[1, c, :].astype(F32)]
-            outs = conv16(six, wt[c, :], False)
-            o = pl.ds(pl.multiple_of(g * GK + i * 16, 16), 16)
-            for r in range(ROWS):
-                mf[c, COLS * r : COLS * (r + 1)] = outs[r]
-                mx[o, COLS * r : COLS * (r + 1)] = outs[r].astype(BF16)
-
-        full = lax.dot_general(
-            kp[at_group(g), COLS : 5 * COLS],
-            mx[at_group(g, GK), :],
-            (((1,), (1,)), ((), ())),
-            preferred_element_type=F32,
-        )
-        put_units(part1, g * UNITS, pack(full))
-        scatter(part1, got1, 0, g)
-
-    send_halos(key_halo)
-    weights_copy = pltpu.make_async_copy(wt, weights_out, out_sem.at[0])
-    weights_copy.start()
-    gather(got1, all1, 0)
+    gather(part1, got1, all1, 0)
     wait_gathered(all1, 0)
 
     @pl.loop(0, groups)
@@ -354,10 +404,10 @@
         packed = take_units(all1, g * UNITS)
         lane = lanes((HD, GK))
         head = lax.shift_right_logical(lane, 5)
-        sums = [packed[:, GC + h : GC + h + 1] for h in range(HPG)]
+        columns = [packed[:, GC + h : GC + h + 1] for h in range(HPG)]
         sums_wide = jnp.zeros((HD, GK), F32)
         for h in range(HPG):
-            sums_wide = jnp.where(head == h, sums[h], sums_wide)
+            sums_wide = jnp.where(head == h, columns[h], sums_wide)
         total = jnp.sum(packed, axis=0, keepdims=True)
         weight = jnp.sum(sums_wide, axis=0, keepdims=True)
         mean = total / (weight + EPS * all_tokens)
@@ -373,7 +423,9 @@
         left = jnp.concatenate([centred, mean_rows], axis=0).astype(BF16)
         cot = cp[at_group(g, GK), :]
         prod = jnp.dot(left, cot, preferred_element_type=F32)
-        stacked = jnp.concatenate([jnp.broadcast_to(s, (HD, 128)) for s in sums], axis=0)
+        vpl[at_group(g), :] = prod[:GC]
+        stacked = jnp.concatenate([jnp.broadcast_to(c, (HD, 128)) for c in columns], axis=0)
+        sums[at_group(g), :] = stacked
         by_head = jnp.where(
             lanes((GC, 128))
             == lax.shift_right_logical(lax.broadcasted_iota(jnp.int32, (GC, 128), 0), 5),
@@ -387,37 +439,44 @@
         both = jnp.dot(
             jnp.concatenate([high, low], axis=0), qa, preferred_element_type=F32
         )
-        denom = both[:16] + both[16:] + EPS * all_tokens
-        inv = 1.0 / denom
+        inv = 1.0 / (both[:8] + both[16:24] + EPS * all_tokens)
+        invs[g] = inv
         down_rows = []
         scaled = []
         for h in range(HPG):
             rows_h = slice(HD * h, HD * h + HD)
             qh = qa[rows_h].astype(F32)
-            ph = prod[rows_h]
-            dot_h = jnp.sum(qh * ph, axis=0, keepdims=True)
+            dot_h = jnp.sum(qh * prod[rows_h], axis=0, keepdims=True)
             inv_h = inv[h : h + 1]
-            down = -(dot_h - EPS * all_tokens * prod[GC + h : GC + h + 1]) * inv_h
-            down_rows.append(down)
-            grad = ph * inv_h + stacked[rows_h, 0:1] * (down * inv_h)
-            grad = jnp.where(qh > 0, grad, 0.0)
+            down_rows.append(
+                -(dot_h - EPS * all_tokens * prod[GC + h : GC + h + 1]) * inv_h
+            )
             scaled.append((qh * inv_h).astype(BF16))
+        down = jnp.concatenate(down_rows + [jnp.zeros((1, ROWS * COLS), F32)], axis=0)
+        downs[g] = down * inv
+        tail = jnp.concatenate([down, jnp.zeros((GK - GC - 8, ROWS * COLS), F32)], axis=0)
+        cp[pl.ds(pl.multiple_of(g * GK + GC, 32), GK - GC), :] = tail.astype(BF16)
+        full = lax.dot_general(
+            jnp.concatenate(scaled, axis=0),
+            cp[at_group(g, GK), :],
+            (((1,), (1,)), ((), ())),
+            preferred_element_type=F32,
+        )
+        put_units(part2, g * UNITS, pack(full))
+        scatter(part2, got2, 1, g)
+
+    @pl.loop(0, groups)
+    def _(g):
+        for h in range(HPG):
+            c = pl.ds(pl.multiple_of(g * GC + h * HD, HD), HD)
             for r in range(ROWS):
-                wide[pl.ds(h * HD * ROWS + r, HD, stride=ROWS), :] = grad[
-                    :, COLS * r : COLS * (r + 1)
-                ]
+                at = slice(COLS * r, COLS * (r + 1))
+                grad = vpl[c, at] * invs[g, h : h + 1, at] + sums[c, :] * downs[g, h : h + 1, at]
+                wide[pl.ds(h * HD * ROWS + r, HD, stride=ROWS), :] = jnp.where(
+                    qp[c, at].astype(F32) > 0, grad, 0.0
+                )
         nat = pl.ds(pl.multiple_of(g * GC * ROWS, GC * ROWS), GC * ROWS)
         qout[nat, :] = wide[...].astype(BF16)
-        tail = jnp.concatenate(down_rows + [jnp.zeros((GK - GC - HPG, ROWS * COLS), F32)], axis=0)
-        right = jnp.concatenate([cot[:GC], tail.astype(BF16)], axis=0)
-        full = lax.dot_general(
-            jnp.concatenate(scaled, axis=0),
-            right,
-            (((1,), (1,)), ((), ())),
-            preferred_element_type=F32,
-        )
-        put_units(part2, g * UNITS, pack(full))
-        scatter(part2, got2, 1, g)
 
     query_copy = pltpu.make_async_copy(qout, query_out, out_sem.at[1])
     query_copy.start()
@@ -434,7 +493,7 @@
     key_copy = pltpu.make_async_copy(kp, key_out, out_sem.at[3])
     key_copy.start()
 
-    gather(got2, all2, 1)
+    gather(part2, got2, all2, 1)
     wait_gathered(all2, 1)
     state_copy = pltpu.make_async_copy(all2, state_out, out_sem.at[4])
     state_copy.start()
@@ -468,7 +527,7 @@
         turned[:, :GC].astype(BF16), keys[...], preferred_element_type=F32
     )
 
-    @pl.loop(0, GC // 16)
+    @pl.loop(0, GC // 16, unroll=UNROLL)
     def _(i):
         c = pl.ds(pl.multiple_of(i * 16, 16), 16)
         six = [mapped[c, COLS * r : COLS * (r + 1)] for r in range(ROWS + 2)]
@@ -496,7 +555,7 @@
             jax.ShapeDtypeStruct((groups * GK, tokens), BF16),
             jax.ShapeDtypeStruct((channels, 6 * COLS), BF16),
             jax.ShapeDtypeStruct(flat, BF16),
-            jax.ShapeDtypeStruct((channels, 128), F32),
+            jax.ShapeDtypeStruct((channels, 9 * COLS), BF16),
         ),
         in_specs=[hbm] * 4 + [pl.BlockSpec(memory_space=pltpu.VMEM)],
         out_specs=(hbm,) * 5,
@@ -515,6 +574,11 @@
             pltpu.VMEM((channels, tokens), F32),
             pltpu.VMEM((groups * GK, tokens), BF16),
             pltpu.VMEM((channels, 128), F32),
+            pltpu.VMEM((channels, 9 * COLS), BF16),
+            pltpu.VMEM((128, 9 * COLS), BF16),
+            pltpu.VMEM((channels, 128), F32),
+            pltpu.VMEM((groups, 8, tokens), F32),
+            pltpu.VMEM((groups, 8, tokens), F32),
             pltpu.VMEM((n_units, *unit), F32),
             pltpu.VMEM((n_units, *unit), F32),
             pltpu.VMEM((2 * n_dev, *unit), F32),
@@ -523,6 +587,7 @@
             pltpu.VMEM((n_units, *unit), F32),
             pltpu.VMEM((groups, 8, GK), F32),
             pltpu.VMEM(flat, BF16),
+            pltpu.SemaphoreType.REGULAR((3,)),
             pltpu.SemaphoreType.DMA((4, groups)),
             pltpu.SemaphoreType.DMA((5,)),
             pltpu.SemaphoreType.DMA((2,)),
@@ -553,7 +618,7 @@
             pl.BlockSpec((UNITS, *unit), lambda g: (g, 0, 0)),
             pl.BlockSpec((GK, tokens), lambda g: (g, 0)),
             pl.BlockSpec((GC, 6 * COLS), lambda g: (g, 0)),
-            pl.BlockSpec((GC, 128), lambda g: (g, 0)),
+            pl.BlockSpec((GC, 9 * COLS), lambda g: (g, 0)),
             nat,
         ],
         out_specs=(nat,) * 3,

time: 115 us -> 80.9 us (0.70)
  Pallas kernels: 114 us -> 79.9 us
    pallas_call x1, Pallas kernels: 85.6 us -> 67.4 us  [shards(): pl.pallas_call(functools.partial(first_kernel, frames, rows, all_tokens),...]
    pallas_call x1, Pallas kernels: 28.8 us -> 12.5 us  [shards(): pl.pallas_call(second_kernel, grid=(groups,), out_shape=(jax.ShapeDtypeSt...]
where the time goes in v2:
time: 80.9 us; the launch traced here: 80.5 us
  Pallas kernels  79.9 us (99%)
    pallas_call x1, Pallas kernels, shards(): pl.pallas_call(functools.partial(first_kernel, frames, rows, all_tokens),...  67.4 us
    pallas_call x1, Pallas kernels, shards(): pl.pallas_call(second_kernel, grid=(groups,), out_shape=(jax.ShapeDtypeSt...  12.5 us

profile of v2, /device:TPU:1, one launch (start us, length us, event | category | flops | bytes accessed | tf_op | source)
XLA Modules:
  0.0 80.5 jit_solution(1537345176142031227)
XLA Ops:
  0.6 67.4 %shard_map.76 = (f32[160,4,128]{2,1,0:T(4,128)}, bf16[2560,512]{1,0:T(8,128)(2,1)}, bf16[2240,768]{1,0:T(8,128)(2,1)}, bf16[8960,128]{1,0:T(8,128)(2,1)}, bf16[2240,1152]{1,0:T(8,128)(2,1)}) custom-call(bf16[8960,128]{1,0:T(8,128)(2,1)} %bitcast.13, bf16[8960,128]{1,0:T(8,128)(2,1)} %bitcast.14, bf16[8960,128]{1,0:T(8,128)(2,1)} %bitcast.15, ...), custom_call_target="tpu_custom_call" | custom-call | tf_op jit(solution)/shard_map/pallas_call | solution.py:551
  68.0 12.5 %shard_map.77 = (bf16[8960,128]{1,0:T(8,128)(2,1)}, bf16[8960,128]{1,0:T(8,128)(2,1)}, bf16[8960,128]{1,0:T(8,128)(2,1)}) custom-call(f32[160,4,128]{2,1,0:T(4,128)} %get-tuple-element.11.state, bf16[2560,512]{1,0:T(8,128)(2,1)} %get-tuple-element.12.mixed, bf16[2240,768]{1,0:T(8,128)(2,1)} %get-tuple-element.13.keys, ...), custom_call_target="tpu_custom_call" | custom-call | tf_op jit(solution)/shard_map/pallas_call | solution.py:613

commit v3 on v2

v3 whole, which is shorter than its diff:
```python
import functools

import jax
import jax.numpy as jnp
from jax import lax
from jax.experimental import pallas as pl
from jax.experimental.pallas import tpu as pltpu
from jax.sharding import PartitionSpec as P

HD = 32
HPG = 7
GC = HPG * HD
GK = 256
COLS = 128
ROWS = 4
UNITS = 8
EPS = 0.001
VMEM_FIRST = 44 * 2**20
VMEM_SECOND = 16 * 2**20
MESH = pl.DeviceIdType.MESH
FLAT = pl.DeviceIdType.LOGICAL
F32 = jnp.float32
BF16 = jnp.bfloat16


def lanes(shape):
    return lax.broadcasted_iota(jnp.int32, shape, len(shape) - 1)


def conv8(rows, taps, flipped):
    outs = []
    for r in range(ROWS):
        sums = []
        for b in range(3):
            total = None
            for a in range(3):
                term = taps[(2 - a) * 3 + 2 - b if flipped else a * 3 + b] * rows[r + a]
                total = term if total is None else total + term
            sums.append(total)
        outs.append(sums[1] + pltpu.roll(sums[0], 1, 1) + pltpu.roll(sums[2], COLS - 1, 1))
    return outs


def one_hot(flipped):
    lane = lanes((128, 9 * COLS))
    tap, at = lax.shift_right_logical(lane, 7), lane & (COLS - 1)
    side = tap - 3 * (tap // 3)
    first, last = (0, COLS - 1) if flipped else (COLS - 1, 0)
    keep = tap == lax.broadcasted_iota(jnp.int32, lane.shape, 0)
    keep = keep & jnp.logical_not((side == 0) & (at == first))
    keep = keep & jnp.logical_not((side == 2) & (at == last))
    return jnp.where(keep, 1.0, 0.0).astype(BF16)


def tap_rows(ref, c):
    return [ref[c, COLS * i : COLS * i + COLS] for i in range(9)]


def pack(full):
    lane = lanes((HD, 128))
    block = lax.shift_right_logical(lane, 5)
    first = jnp.zeros((HD, 128), F32)
    second = jnp.zeros((HD, 128), F32)
    for h in range(HPG):
        rows = slice(HD * h, HD * h + HD)
        if h < 4:
            first = jnp.where(block == h, full[rows, :128], first)
        else:
            second = jnp.where(block == h - 4, full[rows, 128:], second)
        second = jnp.where(lane == 96 + h, full[rows, 128:], second)
    return first, second


def put_units(ref, at, packed):
    for t, part in enumerate(packed):
        for k in range(4):
            ref[at + t * 4 + k] = part[8 * k : 8 * k + 8].astype(ref.dtype)


def take_units(ref, at):
    halves = [
        jnp.concatenate([ref[at + t * 4 + k].astype(F32) for k in range(4)], axis=0)
        for t in range(2)
    ]
    return jnp.concatenate(halves, axis=1)


def spread(packed, keep_sums):
    stacked = jnp.concatenate([packed] * HPG, axis=0)
    head = lax.shift_right_logical(lax.broadcasted_iota(jnp.int32, (GC, GK), 0), 5)
    lane = lanes((GC, GK))
    keep = head == lax.shift_right_logical(lane, 5)
    if keep_sums:
        keep = keep | (lane == GC + head)
    return jnp.where(keep, stacked, 0.0)


def first_kernel(
    frames, rows, all_tokens,
    q_hbm, k_hbm, v_hbm, c_hbm, w_hbm,
    all2, mx, kp, qout, wt,
    qn, kn, vn, cn, wide, vpl, vedge, vhalo, qp, cp, mf, taps0, taps1, hot, sums, invs, downs,
    krows, mrows, part1, part2, got1, got2, all1, means,
    w_ref, here, in_sem, w_sem, vsend, vrecv, ksend, krecv, s_sem, r_sem, g_sem, a_sem,
):
    groups = vpl.shape[0] // GC
    n_dev = frames * rows
    frame, row = lax.axis_index("frame"), lax.axis_index("row")
    me = frame * rows + row
    has_up, has_down = row > 0, row < rows - 1
    n_units = groups * UNITS

    half = n_dev // 2
    even = lax.rem(me, 2) == 0
    owns = even | (lax.rem(me, 8) == 1)
    my_unit = jnp.where(even, me // 2, half + me // 8)
    next_unit = jnp.where(my_unit == n_units - 1, 0, my_unit + 1)
    next_owner = jnp.where(next_unit < half, 2 * next_unit, 8 * (next_unit - half) + 1)

    x, y = frame // 8, lax.rem(frame // 2, 4)
    z, core = lax.rem(frame, 2) + 2 * (row // 2), lax.rem(row, 2)
    xs = [lax.rem(x + i, 4) * 32 for i in range(4)]
    ys = [lax.rem(y + i, 4) * 8 for i in range(4)]
    zs = [lax.rem(z + i, 4) for i in range(4)]
    zs = [lax.rem(a, 2) * 4 + a // 2 * 2 for a in zs]
    zcs = [[a + c for a in zs] for c in (core, 1 - core)]
    steps = [
        (a, b, c, d) for a in range(4) for b in range(4) for c in range(4) for d in range(2)
    ][1:]
    steps.sort(key=lambda step: -sum(min(i, 4 - i) for i in step[:3]))

    def others(act):
        for a, b, c, d in steps:
            act(xs[a] + ys[b] + zcs[d][c])

    sources = ((v_hbm, vn), (k_hbm, kn), (q_hbm, qn), (c_hbm, cn))

    def load(i, g):
        src, dst = sources[i]
        at = pl.ds(pl.multiple_of(g * GC * ROWS, GC * ROWS), GC * ROWS)
        return pltpu.make_async_copy(src.at[at], dst.at[at], in_sem.at[i, g])

    def start_loads(i):
        @pl.loop(0, groups)
        def _(g):
            load(i, g).start()

    start_loads(0)
    barrier = pltpu.get_barrier_semaphore()

    lines = ((1, rows), (rows, 2), (2 * rows, 4), (8 * rows, 4))

    def signal_line(sem, line):
        stride, length = line
        at = lax.rem(me // stride, length)
        for i in range(1, length):
            to = me + (lax.rem(at + i, length) - at) * stride
            pl.semaphore_signal(sem, inc=1, device_id=to, device_id_type=FLAT)

    for line in lines:
        signal_line(barrier, line)
    w_copy = pltpu.make_async_copy(w_hbm, w_ref, w_sem)
    w_copy.start()
    for i in range(1, 4):
        start_loads(i)

    def planes(nat, g):
        at = pl.multiple_of(g * GC * ROWS, GC * ROWS)
        wide[...] = nat[pl.ds(at, GC * ROWS), :].astype(F32)
        return [wide[pl.ds(r, GC, stride=ROWS), :] for r in range(ROWS)]

    def at_group(g, size=GC):
        return pl.ds(pl.multiple_of(g * size, size), size)

    @pl.loop(0, groups)
    def _(g):
        load(0, g).wait()
        rows4 = planes(vn, g)
        for r in range(ROWS):
            vpl[at_group(g), COLS * r : COLS * r + COLS] = rows4[r]
        vedge[0, at_group(g), :] = rows4[0].astype(BF16)
        vedge[1, at_group(g), :] = rows4[3].astype(BF16)

    pl.semaphore_wait(barrier, sum(length - 1 for _, length in lines))
    signal_line(here.at[0], lines[1])

    def value_halo(way, g):
        return pltpu.make_async_remote_copy(
            src_ref=vedge.at[way, at_group(g), :],
            dst_ref=vhalo.at[1 - way, at_group(g), :],
            send_sem=vsend.at[way],
            recv_sem=vrecv.at[1 - way, g],
            device_id=(frame, row - 1 if way == 0 else row + 1),
            device_id_type=MESH,
        )

    def key_halo(way, g):
        src = COLS if way == 0 else 4 * COLS
        dst = 5 * COLS if way == 0 else 0
        return pltpu.make_async_remote_copy(
            src_ref=kp.at[at_group(g), src : src + COLS],
            dst_ref=kp.at[at_group(g), dst : dst + COLS],
            send_sem=ksend.at[way],
            recv_sem=krecv.at[1 - way, g],
            device_id=(frame, row - 1 if way == 0 else row + 1),
            device_id_type=MESH,
        )

    def send_halos(halo):
        for way, there in ((0, has_up), (1, has_down)):

            @pl.when(there)
            def _():
                @pl.loop(0, groups)
                def _(g):
                    halo(way, g).start()

    def wait_halo(halo, g):
        for way, there in ((1, has_up), (0, has_down)):

            @pl.when(there)
            def _():
                halo(way, g).wait_recv()

    def wait_sent(sem):
        for way, there in ((0, has_up), (1, has_down)):

            @pl.when(there)
            def _():
                pltpu.make_async_copy(vedge.at[way], vedge.at[way], sem.at[way]).wait()

    send_halos(value_halo)

    zero_plane = jnp.zeros((GC, COLS), BF16)

    @pl.when(jnp.logical_not(has_up))
    def _():
        @pl.loop(0, groups)
        def _(g):
            vhalo[0, at_group(g), :] = zero_plane
            kp[at_group(g), 0:COLS] = zero_plane

    @pl.when(jnp.logical_not(has_down))
    def _():
        @pl.loop(0, groups)
        def _(g):
            vhalo[1, at_group(g), :] = zero_plane
            kp[at_group(g), 5 * COLS : 6 * COLS] = zero_plane


    @pl.loop(0, groups)
    def _(g):
        load(1, g).wait()
        rows4 = planes(kn, g)
        for r in range(ROWS):
            kp[at_group(g), COLS * (r + 1) : COLS * (r + 2)] = jnp.maximum(
                rows4[r], 0.0
            ).astype(BF16)
        mx[pl.ds(pl.multiple_of(g * GK + GC, 32), GK - GC), :] = jnp.ones(
            (GK - GC, ROWS * COLS), BF16
        )

    w_copy.wait()
    taps = jnp.concatenate([w_ref[a].astype(F32) for a in range(3)], axis=0)
    taps = jnp.concatenate([taps, jnp.zeros((7, taps.shape[1]), F32)], axis=0)
    channels = taps.shape[1]
    for at in range(0, channels, 128):
        size = min(128, channels - at)
        wt[at : at + size, :] = jnp.concatenate(
            [taps[:, at : at + size].T, jnp.zeros((size, 112), F32)], axis=1
        )

    hot[...] = one_hot(False)

    def make_taps(ref, g):
        ref[...] = jnp.dot(
            wt[at_group(g), :].astype(BF16), hot[...], preferred_element_type=F32
        )

    make_taps(taps0, 0)

    for i in range(1, 4):
        pl.semaphore_wait(here.at[i - 1], lines[i][1] - 1)
        if i < 3:
            signal_line(here.at[i], lines[i + 1])

    def scatter(part, got, at, g):
        second = g * UNITS >= half
        start = jnp.where(second, (g * UNITS - half) * 8 + 1, g * UNITS * 2)
        for i in range(UNITS):
            d = start + jnp.where(second, i * 8, i * 2)
            own = d == me
            pltpu.make_async_remote_copy(
                src_ref=part.at[g * UNITS + i],
                dst_ref=got.at[jnp.where(own, n_dev, me)],
                send_sem=s_sem.at[at],
                recv_sem=r_sem.at[at],
                device_id=jnp.where(own, next_owner, d),
                device_id_type=FLAT,
            ).start()

    def wait_bytes(ref, count, sem):
        pltpu.make_async_copy(ref.at[pl.ds(0, count)], ref.at[pl.ds(0, count)], sem).wait()

    def gather(part, got, every, at):
        @pl.when(owns)
        def _():
            wait_bytes(got, n_dev, r_sem.at[at])
            got[me] = part[my_unit]
            total = jnp.sum(got[:n_dev].astype(F32), axis=0)
            every[my_unit] = total.astype(every.dtype)

            def send(d):
                pltpu.make_async_remote_copy(
                    src_ref=every.at[my_unit],
                    dst_ref=every.at[my_unit],
                    send_sem=g_sem.at[at],
                    recv_sem=a_sem.at[at],
                    device_id=d,
                    device_id_type=FLAT,
                ).start()

            others(send)
            wait_bytes(every, n_units - 1, a_sem.at[at])

        @pl.when(jnp.logical_not(owns))
        def _():
            wait_bytes(every, n_units, a_sem.at[at])

    def wait_sends(part, got, at):
        wait_bytes(part, n_units, s_sem.at[at])

        @pl.when(owns)
        def _():
            wait_bytes(got, n_dev - 1, g_sem.at[at])

    def mix(g, taps, next_taps):
        make_taps(next_taps, jnp.minimum(g + 1, groups - 1))
        for i in range(GC // 16):
            c = pl.ds(pl.multiple_of(g * GC + i * 16, 16), 16)
            edge = [vhalo[w, c, :].astype(F32) for w in range(2)]
            both = []
            for k in range(2):
                c8 = pl.ds(pl.multiple_of(g * GC + i * 16 + k * 8, 8), 8)
                six = [edge[0][8 * k : 8 * k + 8]]
                six += [vpl[c8, COLS * r : COLS * (r + 1)] for r in range(ROWS)]
                six += [edge[1][8 * k : 8 * k + 8]]
                outs = conv8(six, tap_rows(taps, slice(i * 16 + k * 8, i * 16 + k * 8 + 8)), False)
                for r in range(ROWS):
                    mf[c8, COLS * r : COLS * (r + 1)] = outs[r]
                both.append(outs)
            o = pl.ds(pl.multiple_of(g * GK + i * 16, 16), 16)
            for r in range(ROWS):
                mx[o, COLS * r : COLS * (r + 1)] = jnp.concatenate(
                    [both[0][r], both[1][r]], axis=0
                ).astype(BF16)
        full = lax.dot_general(
            kp[at_group(g), COLS : 5 * COLS],
            mx[at_group(g, GK), :],
            (((1,), (1,)), ((), ())),
            preferred_element_type=F32,
        )
        put_units(part1, g * UNITS, pack(full))

    @pl.loop(0, groups // 2)
    def _(i):
        wait_halo(value_halo, 2 * i)
        wait_halo(value_halo, 2 * i + 1)
        mix(2 * i, taps0, taps1)
        mix(2 * i + 1, taps1, taps0)
        scatter(part1, got1, 0, 2 * i)
        scatter(part1, got1, 0, 2 * i + 1)

    send_halos(key_halo)
    @pl.loop(0, groups)
    def _(g):
        load(2, g).wait()
        rows4 = planes(qn, g)
        for r in range(ROWS):
            qp[at_group(g), COLS * r : COLS * (r + 1)] = jnp.maximum(rows4[r], 0.0).astype(BF16)

    @pl.loop(0, groups)
    def _(g):
        load(3, g).wait()
        rows4 = planes(cn, g)
        top = pl.ds(pl.multiple_of(g * GK, GK), GC)
        for r in range(ROWS):
            cp[top, COLS * r : COLS * (r + 1)] = rows4[r].astype(BF16)
        cp[pl.ds(pl.multiple_of(g * GK + GC, 32), GK - GC), :] = jnp.zeros(
            (GK - GC, ROWS * COLS), BF16
        )

    gather(part1, got1, all1, 0)

    @pl.loop(0, groups, unroll=2)
    def _(g):
        packed = take_units(all1, g * UNITS)
        lane = lanes((HD, GK))
        head = lax.shift_right_logical(lane, 5)
        columns = [packed[:, GC + h : GC + h + 1] for h in range(HPG)]
        sums_wide = jnp.zeros((HD, GK), F32)
        for h in range(HPG):
            sums_wide = jnp.where(head == h, columns[h], sums_wide)
        total = jnp.sum(packed, axis=0, keepdims=True)
        weight = jnp.sum(sums_wide, axis=0, keepdims=True)
        mean = total / (weight + EPS * all_tokens)
        mean = jnp.where(lanes((1, GK)) < GC, mean, 0.0)
        means[g] = jnp.broadcast_to(mean, (8, GK))
        centred = spread(packed - sums_wide * mean, False)
        mean_rows = jnp.where(
            lax.shift_right_logical(lanes((16, GK)), 5)
            == lax.broadcasted_iota(jnp.int32, (16, GK), 0),
            mean,
            0.0,
        )
        left = jnp.concatenate([centred, mean_rows], axis=0).astype(BF16)
        cot = cp[at_group(g, GK), :]
        prod = jnp.dot(left, cot, preferred_element_type=F32)
        vpl[at_group(g), :] = prod[:GC]
        mrows[g] = prod[GC : GC + 8]
        stacked = jnp.concatenate([jnp.broadcast_to(c, (HD, 128)) for c in columns], axis=0)
        sums[at_group(g), :] = stacked
        by_head = jnp.where(
            lanes((GC, 128))
            == lax.shift_right_logical(lax.broadcasted_iota(jnp.int32, (GC, 128), 0), 5),
            stacked,
            0.0,
        )
        sums_rows = by_head.T[:16]
        high = sums_rows.astype(BF16)
        low = (sums_rows - high.astype(F32)).astype(BF16)
        krows[g] = jnp.concatenate([high, low], axis=0)

    def grads_of_state(g):
        qa = qp[at_group(g), :]
        both = jnp.dot(krows[g], qa, preferred_element_type=F32)
        inv = 1.0 / (both[:8] + both[16:24] + EPS * all_tokens)
        invs[g] = inv
        down_rows = []
        scaled = []
        for h in range(HPG):
            rows_h = slice(HD * h, HD * h + HD)
            qh = qa[rows_h].astype(F32)
            ph = vpl[pl.ds(pl.multiple_of(g * GC + h * HD, HD), HD), :]
            dot_h = jnp.sum(qh * ph, axis=0, keepdims=True)
            inv_h = inv[h : h + 1]
            down_rows.append(
                -(dot_h - EPS * all_tokens * mrows[g, h : h + 1]) * inv_h
            )
            scaled.append((qh * inv_h).astype(BF16))
        down = jnp.concatenate(down_rows + [jnp.zeros((1, ROWS * COLS), F32)], axis=0)
        downs[g] = down * inv
        tail = jnp.concatenate([down, jnp.zeros((GK - GC - 8, ROWS * COLS), F32)], axis=0)
        cp[pl.ds(pl.multiple_of(g * GK + GC, 32), GK - GC), :] = tail.astype(BF16)
        full = lax.dot_general(
            jnp.concatenate(scaled, axis=0),
            cp[at_group(g, GK), :],
            (((1,), (1,)), ((), ())),
            preferred_element_type=F32,
        )
        put_units(part2, g * UNITS, pack(full))

    @pl.loop(0, groups // 2)
    def _(i):
        grads_of_state(2 * i)
        grads_of_state(2 * i + 1)
        scatter(part2, got2, 1, 2 * i)
        scatter(part2, got2, 1, 2 * i + 1)

    @pl.loop(0, groups)
    def _(g):
        for h in range(HPG):
            c = pl.ds(pl.multiple_of(g * GC + h * HD, HD), HD)
            for r in range(ROWS):
                at = slice(COLS * r, COLS * (r + 1))
                grad = vpl[c, at] * invs[g, h : h + 1, at] + sums[c, :] * downs[g, h : h + 1, at]
                wide[pl.ds(h * HD * ROWS + r, HD, stride=ROWS), :] = jnp.where(
                    qp[c, at].astype(F32) > 0, grad, 0.0
                )
        nat = pl.ds(pl.multiple_of(g * GC * ROWS, GC * ROWS), GC * ROWS)
        qout[nat, :] = wide[...].astype(BF16)

    @pl.loop(0, groups)
    def _(g):
        column = means[g].T[:GC, 0:1]
        o = pl.ds(pl.multiple_of(g * GK, GK), GC)
        mx[o, :] = (mf[at_group(g), :] - column).astype(BF16)
        wait_halo(key_halo, g)

    gather(part2, got2, all2, 1)
    wait_sent(vsend)
    wait_sent(ksend)
    wait_sends(part1, got1, 0)
    wait_sends(part2, got2, 1)


def second_kernel(
    state, mixed, keys, weights, query_in, gq, gk, gv, wide, wide2, mapped, hot, taps
):
    g = pl.program_id(0)
    mine = pl.ds(pl.multiple_of(g * GC, GC), GC)
    nat = pl.ds(pl.multiple_of(g * GC * ROWS, GC * ROWS), GC * ROWS)
    mixed = mixed.at[pl.ds(pl.multiple_of(g * GK, GK), GK)]
    keys = keys.at[mine]

    @pl.when(g == 0)
    def _():
        hot[...] = one_hot(True)

    taps[...] = jnp.dot(weights[mine, :].astype(BF16), hot[...], preferred_element_type=F32)
    gq[...] = query_in[nat, :]
    packed = take_units(state, g * UNITS)
    left = spread(packed, True).astype(BF16)
    grad_key = jnp.dot(left, mixed[...], preferred_element_type=F32)
    for r in range(ROWS):
        part = grad_key[:, COLS * r : COLS * (r + 1)]
        wide[pl.ds(r, GC, stride=ROWS), :] = jnp.where(
            keys[:, COLS * (r + 1) : COLS * (r + 2)].astype(F32) > 0, part, 0.0
        )
    gk[...] = wide[...].astype(BF16)
    turned = jnp.concatenate([packed] * 4, axis=0).T[:GC]
    turned = jnp.concatenate([turned, turned], axis=1)
    head = lax.shift_right_logical(lax.broadcasted_iota(jnp.int32, (GC, GK), 0), 5)
    turned = jnp.where(head == lax.shift_right_logical(lanes((GC, GK)), 5), turned, 0.0)
    mapped[...] = jnp.dot(
        turned[:, :GC].astype(BF16), keys[...], preferred_element_type=F32
    )

    for i in range(GC // 8):
        c = slice(8 * i, 8 * i + 8)
        six = [mapped[c, COLS * r : COLS * (r + 1)] for r in range(ROWS + 2)]
        outs = conv8(six, tap_rows(taps, c), True)
        for r in range(ROWS):
            wide2[pl.ds(i * 8 * ROWS + r, 8, stride=ROWS), :] = outs[r]

    gv[...] = wide2[...].astype(BF16)


def shards(frames, rows, query_pre, key_pre, values, cotangent, kernel):
    channels = values.shape[0]
    groups = channels // GC
    flat = (channels * ROWS, COLS)
    tokens = ROWS * COLS
    all_tokens = tokens * frames * rows
    n_units = groups * UNITS
    n_dev = frames * rows
    hbm = pl.BlockSpec(memory_space=pltpu.HBM)
    vmem = pl.BlockSpec(memory_space=pltpu.VMEM)
    unit = (8, 128)
    state, mixed, keys, query, weights = pl.pallas_call(
        functools.partial(first_kernel, frames, rows, all_tokens),
        out_shape=(
            jax.ShapeDtypeStruct((n_units, *unit), BF16),
            jax.ShapeDtypeStruct((groups * GK, tokens), BF16),
            jax.ShapeDtypeStruct((channels, 6 * COLS), BF16),
            jax.ShapeDtypeStruct(flat, BF16),
            jax.ShapeDtypeStruct((channels, 128), F32),
        ),
        in_specs=[hbm] * 5,
        out_specs=(vmem,) * 5,
        scratch_shapes=[
            pltpu.VMEM(flat, BF16),
            pltpu.VMEM(flat, BF16),
            pltpu.VMEM(flat, BF16),
            pltpu.VMEM(flat, BF16),
            pltpu.VMEM((GC * ROWS, COLS), F32),
            pltpu.VMEM((channels, tokens), F32),
            pltpu.VMEM((2, channels, COLS), BF16),
            pltpu.VMEM((2, channels, COLS), BF16),
            pltpu.VMEM((channels, tokens), BF16),
            pltpu.VMEM((groups * GK, tokens), BF16),
            pltpu.VMEM((channels, tokens), F32),
            pltpu.VMEM((GC, 9 * COLS), F32),
            pltpu.VMEM((GC, 9 * COLS), F32),
            pltpu.VMEM((128, 9 * COLS), BF16),
            pltpu.VMEM((channels, 128), F32),
            pltpu.VMEM((groups, 8, tokens), F32),
            pltpu.VMEM((groups, 8, tokens), F32),
            pltpu.VMEM((groups, 32, GC), BF16),
            pltpu.VMEM((groups, 8, tokens), F32),
            pltpu.VMEM((n_units, *unit), F32),
            pltpu.VMEM((n_units, *unit), BF16),
            pltpu.VMEM((n_dev + 1, *unit), F32),
            pltpu.VMEM((n_dev + 1, *unit), BF16),
            pltpu.VMEM((n_units, *unit), F32),
            pltpu.VMEM((groups, 8, GK), F32),
            pltpu.VMEM((3, 3, channels), BF16),
            pltpu.SemaphoreType.REGULAR((3,)),
            pltpu.SemaphoreType.DMA((4, groups)),
            pltpu.SemaphoreType.DMA,
            pltpu.SemaphoreType.DMA((2,)),
            pltpu.SemaphoreType.DMA((2, groups)),
            pltpu.SemaphoreType.DMA((2,)),
            pltpu.SemaphoreType.DMA((2, groups)),
            pltpu.SemaphoreType.DMA((2,)),
            pltpu.SemaphoreType.DMA((2,)),
            pltpu.SemaphoreType.DMA((2,)),
            pltpu.SemaphoreType.DMA((2,)),
        ],
        compiler_params=pltpu.CompilerParams(
            collective_id=0, has_side_effects=True, vmem_limit_bytes=VMEM_FIRST
        ),
    )(
        pltpu.with_memory_space_constraint(query_pre.reshape(flat), pltpu.HBM),
        pltpu.with_memory_space_constraint(key_pre.reshape(flat), pltpu.HBM),
        pltpu.with_memory_space_constraint(values.reshape(flat), pltpu.HBM),
        pltpu.with_memory_space_constraint(cotangent.reshape(flat), pltpu.HBM),
        pltpu.with_memory_space_constraint(kernel, pltpu.HBM),
    )
    nat = pl.BlockSpec((GC * ROWS, COLS), lambda g: (g, 0))
    gq, gk, gv = pl.pallas_call(
        second_kernel,
        grid=(groups,),
        out_shape=(jax.ShapeDtypeStruct(flat, BF16),) * 3,
        in_specs=[vmem] * 5,
        out_specs=(nat,) * 3,
        scratch_shapes=[
            pltpu.VMEM((GC * ROWS, COLS), F32),
            pltpu.VMEM((GC * ROWS, COLS), F32),
            pltpu.VMEM((GC, 6 * COLS), F32),
            pltpu.VMEM((128, 9 * COLS), BF16),
            pltpu.VMEM((GC, 9 * COLS), F32),
        ],
        compiler_params=pltpu.CompilerParams(vmem_limit_bytes=VMEM_SECOND),
    )(state, mixed, keys, weights, query)
    return tuple(o.reshape(values.shape) for o in (gq, gk, gv))


def solution(mesh):
    frames, rows = mesh.shape["frame"], mesh.shape["row"]
    spec = P(None, "frame", "row", None)
    return jax.shard_map(
        functools.partial(shards, frames, rows),
        mesh=mesh,
        in_specs=(spec, spec, spec, spec, P()),
        out_specs=(spec, spec, spec),
        check_vma=False,
    )
```

time: 80.9 us -> 67.4 us (0.83)
  Pallas kernels: 79.9 us -> 66.7 us
    pallas_call x1, Pallas kernels: 67.4 us -> 57.9 us  [shards(): pl.pallas_call(functools.partial(first_kernel, frames, rows, all_tokens),...]
    pallas_call x1, Pallas kernels: 12.5 us -> 8.79 us  [shards(): pl.pallas_call(second_kernel, grid=(groups,), out_shape=(jax.ShapeDtypeSt...]
where the time goes in v3:
time: 67.4 us; the launch traced here: 67.3 us
  Pallas kernels  66.7 us (99%)
    pallas_call x1, Pallas kernels, shards(): pl.pallas_call(functools.partial(first_kernel, frames, rows, all_tokens),...  57.9 us
    pallas_call x1, Pallas kernels, shards(): pl.pallas_call(second_kernel, grid=(groups,), out_shape=(jax.ShapeDtypeSt...  8.79 us

profile of v3, /device:TPU:1, one launch (start us, length us, event | category | flops | bytes accessed | tf_op | source)
XLA Modules:
  0.0 67.3 jit_solution(15555415703733017286)
XLA Ops:
  0.6 57.9 %shard_map.76 = (bf16[80,8,128]{2,1,0:T(8,128)(2,1)S(1)}, bf16[2560,512]{1,0:T(8,128)(2,1)S(1)}, bf16[2240,768]{1,0:T(8,128)(2,1)S(1)}, bf16[8960,128]{1,0:T(8,128)(2,1)S(1)}, f32[2240,128]{1,0:T(8,128)S(1)}) custom-call(bf16[8960,128]{1,0:T(8,128)(2,1)} %bitcast.13, bf16[8960,128]{1,0:T(8,128)(2,1)} %bitcast.14, bf16[8960,128]{1,0:T(8,128)(2,1)} %bitcast.15, ...), custom_call_target="tpu_custom_call" | custom-call | tf_op jit(solution)/shard_map/pallas_call | solution.py:550
  58.5 8.8 %shard_map.77 = (bf16[8960,128]{1,0:T(8,128)(2,1)}, bf16[8960,128]{1,0:T(8,128)(2,1)}, bf16[8960,128]{1,0:T(8,128)(2,1)}) custom-call(bf16[80,8,128]{2,1,0:T(8,128)(2,1)S(1)} %get-tuple-element.11.state, bf16[2560,512]{1,0:T(8,128)(2,1)S(1)} %get-tuple-element.12.mixed, bf16[2240,768]{1,0:T(8,128)(2,1)S(1)} %get-tuple-element.13.keys, ...), custom_call_target="tpu_custom_call" | custom-call | tf_op jit(solution)/shard_map/pallas_call | solution.py:611

commit v4 on v3

--- a/solution.py
+++ b/solution.py
@@ -371,7 +371,6 @@
         scatter(part1, got1, 0, 2 * i)
         scatter(part1, got1, 0, 2 * i + 1)
 
-    send_halos(key_halo)
     @pl.loop(0, groups)
     def _(g):
         load(2, g).wait()
@@ -467,6 +466,8 @@
         scatter(part2, got2, 1, 2 * i)
         scatter(part2, got2, 1, 2 * i + 1)
 
+    send_halos(key_halo)
+
     @pl.loop(0, groups)
     def _(g):
         for h in range(HPG):
@@ -485,9 +486,12 @@
         column = means[g].T[:GC, 0:1]
         o = pl.ds(pl.multiple_of(g * GK, GK), GC)
         mx[o, :] = (mf[at_group(g), :] - column).astype(BF16)
+    gather(part2, got2, all2, 1)
+
+    @pl.loop(0, groups)
+    def _(g):
         wait_halo(key_halo, g)
 
-    gather(part2, got2, all2, 1)
     wait_sent(vsend)
     wait_sent(ksend)
     wait_sends(part1, got1, 0)

time: 67.4 us -> 61.7 us (0.915)
  Pallas kernels: 66.7 us -> 60.9 us
    pallas_call x1, Pallas kernels: 57.9 us -> 52.1 us  [shards(): pl.pallas_call(functools.partial(first_kernel, frames, rows, all_tokens),...]
where the time goes in v4:
time: 61.7 us; the launch traced here: 61.6 us
  Pallas kernels  60.9 us (99%)
  between operations  0.64 us (1%)
    pallas_call x1, Pallas kernels, shards(): pl.pallas_call(functools.partial(first_kernel, frames, rows, all_tokens),...  52.1 us
    pallas_call x1, Pallas kernels, shards(): pl.pallas_call(second_kernel, grid=(groups,), out_shape=(jax.ShapeDtypeSt...  8.8 us

profile of v4, /device:TPU:1, one launch (start us, length us, event | category | flops | bytes accessed | tf_op | source)
XLA Modules:
  0.0 61.6 jit_solution(8602504749828313609)
XLA Ops:
  0.6 52.1 %shard_map.76 = (bf16[80,8,128]{2,1,0:T(8,128)(2,1)S(1)}, bf16[2560,512]{1,0:T(8,128)(2,1)S(1)}, bf16[2240,768]{1,0:T(8,128)(2,1)S(1)}, bf16[8960,128]{1,0:T(8,128)(2,1)S(1)}, f32[2240,128]{1,0:T(8,128)S(1)}) custom-call(bf16[8960,128]{1,0:T(8,128)(2,1)} %bitcast.13, bf16[8960,128]{1,0:T(8,128)(2,1)} %bitcast.14, bf16[8960,128]{1,0:T(8,128)(2,1)} %bitcast.15, ...), custom_call_target="tpu_custom_call" | custom-call | tf_op jit(solution)/shard_map/pallas_call | solution.py:554
  52.8 8.8 %shard_map.77 = (bf16[8960,128]{1,0:T(8,128)(2,1)}, bf16[8960,128]{1,0:T(8,128)(2,1)}, bf16[8960,128]{1,0:T(8,128)(2,1)}) custom-call(bf16[80,8,128]{2,1,0:T(8,128)(2,1)S(1)} %get-tuple-element.11.state, bf16[2560,512]{1,0:T(8,128)(2,1)S(1)} %get-tuple-element.12.mixed, bf16[2240,768]{1,0:T(8,128)(2,1)S(1)} %get-tuple-element.13.keys, ...), custom_call_target="tpu_custom_call" | custom-call | tf_op jit(solution)/shard_map/pallas_call | solution.py:615

commit v5 on v4

--- a/solution.py
+++ b/solution.py
@@ -77,9 +77,9 @@
             ref[at + t * 4 + k] = part[8 * k : 8 * k + 8].astype(ref.dtype)
 
 
-def take_units(ref, at):
+def take_units(ref, at, apart=4):
     halves = [
-        jnp.concatenate([ref[at + t * 4 + k].astype(F32) for k in range(4)], axis=0)
+        jnp.concatenate([ref[at + t * apart + k].astype(F32) for k in range(4)], axis=0)
         for t in range(2)
     ]
     return jnp.concatenate(halves, axis=1)
@@ -100,8 +100,9 @@
     q_hbm, k_hbm, v_hbm, c_hbm, w_hbm,
     all2, mx, kp, qout, wt,
     qn, kn, vn, cn, wide, vpl, vedge, vhalo, qp, cp, mf, taps0, taps1, hot, sums, invs, downs,
-    krows, mrows, part1, part2, got1, got2, all1, means,
+    krows, mrows, part1, part2, got1, got2, all1, means, pair, both, yard,
     w_ref, here, in_sem, w_sem, vsend, vrecv, ksend, krecv, s_sem, r_sem, g_sem, a_sem,
+    pair_send, pair_recv,
 ):
     groups = vpl.shape[0] // GC
     n_dev = frames * rows
@@ -129,9 +130,23 @@
     ][1:]
     steps.sort(key=lambda step: -sum(min(i, 4 - i) for i in step[:3]))
 
-    def others(act):
+    def others(act, same_core=False):
         for a, b, c, d in steps:
-            act(xs[a] + ys[b] + zcs[d][c])
+            if not (same_core and d):
+                act(xs[a] + ys[b] + zcs[d][c])
+
+    chips, n_half = n_dev // 2, n_units // 2
+    chip, partner = me // 2, me + 1 - 2 * core
+    order = lax.rem(13 * chip, chips)
+    again = n_units - chips
+    owns_piece = jnp.where(core == 0, order < n_half, (order >= n_half) | (order < again))
+    wrapped = jnp.where(order >= n_half, order - n_half, order + chips - n_half)
+    my_piece = jnp.where(core == 0, order, wrapped)
+
+    def piece_owner(v):
+        return 2 * lax.rem(5 * (v + n_half * core), chips) + core
+
+    next_piece = piece_owner(jnp.where(my_piece == n_half - 1, 0, my_piece + 1))
 
     sources = ((v_hbm, vn), (k_hbm, kn), (q_hbm, qn), (c_hbm, cn))
 
@@ -299,6 +314,58 @@
                 device_id_type=FLAT,
             ).start()
 
+    def pair_copy(g):
+        return pltpu.make_async_remote_copy(
+            src_ref=part1.at[pl.ds(g * UNITS + 4 * (1 - core), 4)],
+            dst_ref=pair.at[pl.ds(g * 4, 4)],
+            send_sem=pair_send,
+            recv_sem=pair_recv.at[g],
+            device_id=partner,
+            device_id_type=FLAT,
+        )
+
+    def scatter_pieces(g):
+        pair_copy(g).wait_recv()
+        for k in range(4):
+            both[g * 4 + k] = part1[g * UNITS + 4 * core + k] + pair[g * 4 + k]
+        for k in range(4):
+            d = piece_owner(g * 4 + k)
+            own = d == me
+            pltpu.make_async_remote_copy(
+                src_ref=both.at[g * 4 + k],
+                dst_ref=got1.at[jnp.where(own, chips, chip)],
+                send_sem=s_sem.at[0],
+                recv_sem=r_sem.at[0],
+                device_id=jnp.where(own, next_piece, d),
+                device_id_type=FLAT,
+            ).start()
+
+    def gather_pieces():
+        at = core * n_half + my_piece
+
+        @pl.when(owns_piece)
+        def _():
+            wait_bytes(got1, chips, r_sem.at[0])
+            got1[chip] = both[my_piece]
+            all1[at] = jnp.sum(got1[:chips], axis=0)
+
+            def send(d):
+                pltpu.make_async_remote_copy(
+                    src_ref=all1.at[at],
+                    dst_ref=all1.at[at],
+                    send_sem=g_sem.at[0],
+                    recv_sem=a_sem.at[0],
+                    device_id=d,
+                    device_id_type=FLAT,
+                ).start()
+
+            others(send)
+            wait_bytes(all1, n_units - 1, a_sem.at[0])
+
+        @pl.when(jnp.logical_not(owns_piece))
+        def _():
+            wait_bytes(all1, n_units, a_sem.at[0])
+
     def wait_bytes(ref, count, sem):
         pltpu.make_async_copy(ref.at[pl.ds(0, count)], ref.at[pl.ds(0, count)], sem).wait()
 
@@ -327,19 +394,25 @@
         def _():
             wait_bytes(every, n_units, a_sem.at[at])
 
-    def wait_sends(part, got, at):
-        wait_bytes(part, n_units, s_sem.at[at])
+    def wait_sends():
+        wait_bytes(pair, n_half, pair_send)
+        wait_bytes(both, n_half, s_sem.at[0])
+        wait_bytes(part2, n_units, s_sem.at[1])
+
+        @pl.when(owns_piece)
+        def _():
+            wait_bytes(yard, n_dev - 1, g_sem.at[0])
 
         @pl.when(owns)
         def _():
-            wait_bytes(got, n_dev - 1, g_sem.at[at])
+            wait_bytes(got2, n_dev - 1, g_sem.at[1])
 
     def mix(g, taps, next_taps):
         make_taps(next_taps, jnp.minimum(g + 1, groups - 1))
         for i in range(GC // 16):
             c = pl.ds(pl.multiple_of(g * GC + i * 16, 16), 16)
             edge = [vhalo[w, c, :].astype(F32) for w in range(2)]
-            both = []
+            pieces = []
             for k in range(2):
                 c8 = pl.ds(pl.multiple_of(g * GC + i * 16 + k * 8, 8), 8)
                 six = [edge[0][8 * k : 8 * k + 8]]
@@ -348,11 +421,11 @@
                 outs = conv8(six, tap_rows(taps, slice(i * 16 + k * 8, i * 16 + k * 8 + 8)), False)
                 for r in range(ROWS):
                     mf[c8, COLS * r : COLS * (r + 1)] = outs[r]
-                both.append(outs)
+                pieces.append(outs)
             o = pl.ds(pl.multiple_of(g * GK + i * 16, 16), 16)
             for r in range(ROWS):
                 mx[o, COLS * r : COLS * (r + 1)] = jnp.concatenate(
-                    [both[0][r], both[1][r]], axis=0
+                    [pieces[0][r], pieces[1][r]], axis=0
                 ).astype(BF16)
         full = lax.dot_general(
             kp[at_group(g), COLS : 5 * COLS],
@@ -368,8 +441,16 @@
         wait_halo(value_halo, 2 * i + 1)
         mix(2 * i, taps0, taps1)
         mix(2 * i + 1, taps1, taps0)
-        scatter(part1, got1, 0, 2 * i)
-        scatter(part1, got1, 0, 2 * i + 1)
+        pair_copy(2 * i).start()
+        pair_copy(2 * i + 1).start()
+
+        @pl.when(i > 0)
+        def _():
+            scatter_pieces(2 * i - 2)
+            scatter_pieces(2 * i - 1)
+
+    scatter_pieces(groups - 2)
+    scatter_pieces(groups - 1)
 
     @pl.loop(0, groups)
     def _(g):
@@ -389,11 +470,11 @@
             (GK - GC, ROWS * COLS), BF16
         )
 
-    gather(part1, got1, all1, 0)
+    gather_pieces()
 
     @pl.loop(0, groups, unroll=2)
     def _(g):
-        packed = take_units(all1, g * UNITS)
+        packed = take_units(all1, g * 4, n_half)
         lane = lanes((HD, GK))
         head = lax.shift_right_logical(lane, 5)
         columns = [packed[:, GC + h : GC + h + 1] for h in range(HPG)]
@@ -432,8 +513,8 @@
 
     def grads_of_state(g):
         qa = qp[at_group(g), :]
-        both = jnp.dot(krows[g], qa, preferred_element_type=F32)
-        inv = 1.0 / (both[:8] + both[16:24] + EPS * all_tokens)
+        denoms = jnp.dot(krows[g], qa, preferred_element_type=F32)
+        inv = 1.0 / (denoms[:8] + denoms[16:24] + EPS * all_tokens)
         invs[g] = inv
         down_rows = []
         scaled = []
@@ -494,8 +575,7 @@
 
     wait_sent(vsend)
     wait_sent(ksend)
-    wait_sends(part1, got1, 0)
-    wait_sends(part2, got2, 1)
+    wait_sends()
 
 
 def second_kernel(
@@ -584,10 +664,13 @@
             pltpu.VMEM((groups, 8, tokens), F32),
             pltpu.VMEM((n_units, *unit), F32),
             pltpu.VMEM((n_units, *unit), BF16),
-            pltpu.VMEM((n_dev + 1, *unit), F32),
+            pltpu.VMEM((n_dev // 2 + 1, *unit), F32),
             pltpu.VMEM((n_dev + 1, *unit), BF16),
             pltpu.VMEM((n_units, *unit), F32),
             pltpu.VMEM((groups, 8, GK), F32),
+            pltpu.VMEM((n_units // 2, *unit), F32),
+            pltpu.VMEM((n_units // 2, *unit), F32),
+            pltpu.VMEM((n_dev, *unit), F32),
             pltpu.VMEM((3, 3, channels), BF16),
             pltpu.SemaphoreType.REGULAR((3,)),
             pltpu.SemaphoreType.DMA((4, groups)),
@@ -600,6 +683,8 @@
             pltpu.SemaphoreType.DMA((2,)),
             pltpu.SemaphoreType.DMA((2,)),
             pltpu.SemaphoreType.DMA((2,)),
+            pltpu.SemaphoreType.DMA,
+            pltpu.SemaphoreType.DMA((groups,)),
         ],
         compiler_params=pltpu.CompilerParams(
             collective_id=0, has_side_effects=True, vmem_limit_bytes=VMEM_FIRST

time: 61.7 us -> 60.3 us (0.977)
  Pallas kernels: 60.9 us -> 59.5 us
    pallas_call x1, Pallas kernels: 52.1 us -> 50.7 us  [shards(): pl.pallas_call(functools.partial(first_kernel, frames, rows, all_tokens),...]
where the time goes in v5:
time: 60.3 us; the launch traced here: 60.2 us
  Pallas kernels  59.5 us (99%)
  between operations  0.64 us (1%)
    pallas_call x1, Pallas kernels, shards(): pl.pallas_call(functools.partial(first_kernel, frames, rows, all_tokens),...  50.7 us
    pallas_call x1, Pallas kernels, shards(): pl.pallas_call(second_kernel, grid=(groups,), out_shape=(jax.ShapeDtypeSt...  8.8 us

profile of v5, /device:TPU:1, one launch (start us, length us, event | category | flops | bytes accessed | tf_op | source)
XLA Modules:
  0.0 60.2 jit_solution(13127223509643721876)
XLA Ops:
  0.6 50.7 %shard_map.76 = (bf16[80,8,128]{2,1,0:T(8,128)(2,1)S(1)}, bf16[2560,512]{1,0:T(8,128)(2,1)S(1)}, bf16[2240,768]{1,0:T(8,128)(2,1)S(1)}, bf16[8960,128]{1,0:T(8,128)(2,1)S(1)}, f32[2240,128]{1,0:T(8,128)S(1)}) custom-call(bf16[8960,128]{1,0:T(8,128)(2,1)} %bitcast.13, bf16[8960,128]{1,0:T(8,128)(2,1)} %bitcast.14, bf16[8960,128]{1,0:T(8,128)(2,1)} %bitcast.15, ...), custom_call_target="tpu_custom_call" | custom-call | tf_op jit(solution)/shard_map/pallas_call | solution.py:634
  51.4 8.8 %shard_map.77 = (bf16[8960,128]{1,0:T(8,128)(2,1)}, bf16[8960,128]{1,0:T(8,128)(2,1)}, bf16[8960,128]{1,0:T(8,128)(2,1)}) custom-call(bf16[80,8,128]{2,1,0:T(8,128)(2,1)S(1)} %get-tuple-element.11.state, bf16[2560,512]{1,0:T(8,128)(2,1)S(1)} %get-tuple-element.12.mixed, bf16[2240,768]{1,0:T(8,128)(2,1)S(1)} %get-tuple-element.13.keys, ...), custom_call_target="tpu_custom_call" | custom-call | tf_op jit(solution)/shard_map/pallas_call | solution.py:700

commit v6 on v5

--- a/solution.py
+++ b/solution.py
@@ -161,6 +161,7 @@
             load(i, g).start()
 
     start_loads(0)
+    hot[...] = one_hot(False)
     barrier = pltpu.get_barrier_semaphore()
 
     lines = ((1, rows), (rows, 2), (2 * rows, 4), (8 * rows, 4))
@@ -284,8 +285,6 @@
         wt[at : at + size, :] = jnp.concatenate(
             [taps[:, at : at + size].T, jnp.zeros((size, 112), F32)], axis=1
         )
-
-    hot[...] = one_hot(False)
 
     def make_taps(ref, g):
         ref[...] = jnp.dot(
@@ -472,7 +471,7 @@
 
     gather_pieces()
 
-    @pl.loop(0, groups, unroll=2)
+    @pl.loop(0, groups, unroll=5)
     def _(g):
         packed = take_units(all1, g * 4, n_half)
         lane = lanes((HD, GK))
@@ -540,12 +539,12 @@
         )
         put_units(part2, g * UNITS, pack(full))
 
-    @pl.loop(0, groups // 2)
+    @pl.loop(0, groups // 5)
     def _(i):
-        grads_of_state(2 * i)
-        grads_of_state(2 * i + 1)
-        scatter(part2, got2, 1, 2 * i)
-        scatter(part2, got2, 1, 2 * i + 1)
+        for k in range(5):
+            grads_of_state(5 * i + k)
+        for k in range(5):
+            scatter(part2, got2, 1, 5 * i + k)
 
     send_halos(key_halo)
 

time: 60.3 us -> 59.9 us (level)
  no operation moved by 1% of the time
where the time goes in v6:
time: 59.9 us; the launch traced here: 59.8 us
  Pallas kernels  59.2 us (99%)
  between operations  0.64 us (1%)
    pallas_call x1, Pallas kernels, shards(): pl.pallas_call(functools.partial(first_kernel, frames, rows, all_tokens),...  50.4 us
    pallas_call x1, Pallas kernels, shards(): pl.pallas_call(second_kernel, grid=(groups,), out_shape=(jax.ShapeDtypeSt...  8.79 us

profile of v6, /device:TPU:1, one launch (start us, length us, event | category | flops | bytes accessed | tf_op | source)
XLA Modules:
  0.0 59.8 jit_solution(12927353298950664426)
XLA Ops:
  0.6 50.4 %shard_map.76 = (bf16[80,8,128]{2,1,0:T(8,128)(2,1)S(1)}, bf16[2560,512]{1,0:T(8,128)(2,1)S(1)}, bf16[2240,768]{1,0:T(8,128)(2,1)S(1)}, bf16[8960,128]{1,0:T(8,128)(2,1)S(1)}, f32[2240,128]{1,0:T(8,128)S(1)}) custom-call(bf16[8960,128]{1,0:T(8,128)(2,1)} %bitcast.13, bf16[8960,128]{1,0:T(8,128)(2,1)} %bitcast.14, bf16[8960,128]{1,0:T(8,128)(2,1)} %bitcast.15, ...), custom_call_target="tpu_custom_call" | custom-call | tf_op jit(solution)/shard_map/pallas_call | solution.py:633
  51.0 8.8 %shard_map.77 = (bf16[8960,128]{1,0:T(8,128)(2,1)}, bf16[8960,128]{1,0:T(8,128)(2,1)}, bf16[8960,128]{1,0:T(8,128)(2,1)}) custom-call(bf16[80,8,128]{2,1,0:T(8,128)(2,1)S(1)} %get-tuple-element.11.state, bf16[2560,512]{1,0:T(8,128)(2,1)S(1)} %get-tuple-element.12.mixed, bf16[2240,768]{1,0:T(8,128)(2,1)S(1)} %get-tuple-element.13.keys, ...), custom_call_target="tpu_custom_call" | custom-call | tf_op jit(solution)/shard_map/pallas_call | solution.py:699
